TPU v7x, 32 devices: a whole 2x2x4 slice. The times are simulated.
32 devices in a mesh: grp: 4 (over z), shard: 8 (over y, x, core).
Axes of the slice: x: 2, y: 2, z: 4, core: 2. Of those that a mesh axis runs over, the one named last changes fastest.
Arguments:
- latents: bfloat16 [4096, 1024], P(('grp', 'shard')), may hold values from -6 to 6
- head_weight: bfloat16 [1024, 1024], P('shard'), may hold values from -0.1875 to 0.1875
- norm_gain: float32 [1024], replicated, may hold values from 0.1 to 1.9
- color_head: bfloat16 [4, 256], replicated, may hold values from -1.5 to 1.5
- sample_points: float32 [2048, 192], P(('grp', 'shard')), may hold values from -1 to 1
- sample_spacing: float32 [2048, 64], P(('grp', 'shard')), may hold values from 0.002 to 0.02
- ray_targets: float32 [3, 2048], P(None, ('grp', 'shard')), may hold values from 0 to 1
- ray_scene: int32 [2048], P(('grp', 'shard')), may hold values from 0 to 31, as said below
Outputs:
- rendered_color: float32 [3, 2048], P(None, ('grp', 'shard'))
- loss: float32 [], replicated
- head_grad: float32 [1024, 1024], P('shard')
- norm_gain_grad: float32 [1024], replicated
- latent_grad: bfloat16 [4096, 1024], P(('grp', 'shard'))
Inputs may be any that keep to these rules, and one draw needn't show every extreme that they name: `ray_scene`: one scene, drawn from the seed, is named by exactly 8 rays of every device; no device names any scene more than 8 times; every scene is named by one ray or more, and the totals of the other scenes differ from one another by one at most.
All inputs are finite; a program needn't handle non-finite values.
Results may differ from a plain program's by a relative error of at most 0.017.
Values may be sent and summed in bfloat16 or wider, within the bound.
A program may use at most 64 MiB of HBM per device.

v0:
```python
import functools

import jax
import jax.numpy as jnp
from jax import lax
from jax.experimental import pallas as pl
from jax.experimental.pallas import tpu as pltpu
from jax.sharding import PartitionSpec as P

norm_eps = 1e-06


LANES = 128
HALVES = 2
SINE = (3.14159265358979, -5.16771278004997, 2.55016403987735, -0.599264529320792, 0.0821458866111282, -0.00737043094571435, 0.000466302805767613, -0.0000219153534478303)


def sine_of_pi(turns):
    whole = jnp.floor(turns + 0.5)
    rest = turns - whole
    odd = whole - 2.0 * jnp.floor(whole * 0.5)
    square = rest * rest
    value = jnp.full_like(square, SINE[-1])
    for coefficient in SINE[-2::-1]:
        value = value * square + coefficient
    return value * (rest * (1.0 - 2.0 * odd))


def ray_kernel(
    ray_depth,
    points_ref,
    spacing_ref,
    target_ref,
    factor_ref,
    first_ref,
    second_ref,
    head_ref,
    color_ref,
    loss_ref,
    d_first_ref,
    d_second_ref,
    first_t_ref,
    second_t_ref,
    grad_first_ref,
    grad_second_ref,
    raw_ref,
    draw_ref,
):
    width = second_ref.shape[0]
    fan_scale = width ** (-0.5)
    samples = points_ref.shape[1]
    chunks = samples // LANES

    @pl.when(pl.program_id(0) == 0)
    def _():
        loss_ref[...] = jnp.zeros_like(loss_ref)
        grad_first_ref[...] = jnp.zeros_like(grad_first_ref)
        grad_second_ref[...] = jnp.zeros_like(grad_second_ref)
        first_t_ref[...] = first_ref[...].T
        second_t_ref[...] = second_ref[...].T

    feature = lax.broadcasted_iota(jnp.int32, (48, 1), 0)
    component = feature % 3
    scale = jnp.exp2((feature // 6 % 8).astype(jnp.float32))
    phase = (feature // 3 % 2).astype(jnp.float32) * 0.5
    picked = jnp.where(
        component == 0,
        points_ref[0:1, :],
        jnp.where(component == 1, points_ref[1:2, :], points_ref[2:3, :]),
    )
    turns = picked * scale
    turns = turns - 2.0 * jnp.floor(turns * 0.5)
    distinct = sine_of_pi(turns + phase).astype(jnp.bfloat16)
    copies = width // 48
    h_zero = jnp.concatenate([distinct] * copies + [distinct[: width - 48 * copies]], axis=0)

    def product(a, b):
        return jnp.dot(a, b, preferred_element_type=jnp.float32)

    h_one = jnp.maximum(product(first_t_ref[...], h_zero) * fan_scale, 0.0).astype(jnp.bfloat16)
    h_two = jnp.maximum(product(second_t_ref[...], h_one) * fan_scale, 0.0).astype(jnp.bfloat16)
    raw = product(head_ref[...], h_two)
    for i in range(chunks):
        for c in range(4):
            raw_ref[c, i : i + 1, :] = raw[c : c + 1, i * LANES : (i + 1) * LANES]

    row = lax.broadcasted_iota(jnp.int32, (LANES, LANES), 0)
    column = lax.broadcasted_iota(jnp.int32, (LANES, LANES), 1)
    same = row // ray_depth == column // ray_depth
    before_sum = jnp.where(jnp.logical_and(same, row < column), 1.0, 0.0)
    behind_sum = jnp.where(jnp.logical_and(same, row > column), 1.0, 0.0)
    whole_sum = jnp.where(same, 1.0, 0.0)

    def along(values, matrix):
        return jnp.dot(
            values, matrix, preferred_element_type=jnp.float32, precision=lax.Precision.HIGHEST
        )

    spacing = spacing_ref[...]
    factor = factor_ref[...]
    density_raw = raw_ref[0]
    density = jnp.maximum(density_raw, 0.0) + jnp.log1p(jnp.exp(-jnp.abs(density_raw)))
    optical = density * spacing
    transmit = jnp.exp(-along(optical, before_sum))
    survive = jnp.exp(-optical)
    blend = transmit * (1.0 - survive)
    d_blend = jnp.zeros_like(blend)
    loss = jnp.zeros_like(blend)
    tints = []
    for c in range(3):
        albedo = 1.0 / (1.0 + jnp.exp(-raw_ref[c + 1]))
        color = along(blend * (albedo - 1.0), whole_sum) + 1.0
        color_ref[c] = color
        residual = color - target_ref[c]
        loss = loss + residual * residual
        grad_color = 2.0 * residual * factor
        d_blend = d_blend + grad_color * (albedo - 1.0)
        tints.append(grad_color * blend * albedo * (1.0 - albedo))
    loss_ref[...] += loss * factor
    behind = along(d_blend * blend, behind_sum)
    d_optical = d_blend * transmit * survive - behind
    d_density = d_optical * spacing * (1.0 / (1.0 + jnp.exp(-density_raw)))
    for c, value in enumerate([d_density] + tints):
        for i in range(chunks):
            draw_ref[c : c + 1, i * LANES : (i + 1) * LANES] = value[i : i + 1, :]
    d_raw = draw_ref[...].astype(jnp.bfloat16)
    d_htwo = lax.dot_general(
        head_ref[...], d_raw, (((0,), (0,)), ((), ())), preferred_element_type=jnp.float32
    )
    d_atwo = (jnp.where(h_two > 0, d_htwo, 0.0) * fan_scale).astype(jnp.bfloat16)
    over_samples = (((1,), (1,)), ((), ()))
    grad_second_ref[...] += lax.dot_general(
        h_one, d_atwo, over_samples, preferred_element_type=jnp.float32
    )
    d_hone = product(second_ref[...], d_atwo)
    d_aone = (jnp.where(h_one > 0, d_hone, 0.0) * fan_scale).astype(jnp.bfloat16)
    grad_first_ref[...] += lax.dot_general(
        distinct, d_aone, over_samples, preferred_element_type=jnp.float32
    )

    @pl.when(pl.program_id(0) == pl.num_programs(0) - 1)
    def _():
        first = grad_first_ref[...].astype(jnp.bfloat16)
        d_first_ref[...] = jnp.concatenate([first] * copies + [first[: width - 48 * copies]], axis=0)
        d_second_ref[...] = grad_second_ref[...].astype(jnp.bfloat16)


def render_slots(points, spacing, target, factor, w_first, w_second, color_head):
    slots, ray_depth = spacing.shape
    width = w_first.shape[0]
    total = slots * ray_depth
    block = 2048
    rows = total // LANES
    block_rows = block // LANES
    flat_points = points.reshape(slots, 3, ray_depth).transpose(1, 0, 2).reshape(3, total)
    wide_target = jnp.broadcast_to(target.T[:, :, None], (3, slots, ray_depth)).reshape(3, rows, LANES)
    wide_factor = jnp.broadcast_to(factor[:, None], (slots, ray_depth)).reshape(rows, LANES)
    fixed = lambda b: (0, 0)
    color, loss, grad_first, grad_second = pl.pallas_call(
        functools.partial(ray_kernel, ray_depth),
        grid=(total // block,),
        in_specs=[
            pl.BlockSpec((3, block), lambda b: (0, b)),
            pl.BlockSpec((block_rows, LANES), lambda b: (b, 0)),
            pl.BlockSpec((3, block_rows, LANES), lambda b: (0, b, 0)),
            pl.BlockSpec((block_rows, LANES), lambda b: (b, 0)),
            pl.BlockSpec((width, width), fixed),
            pl.BlockSpec((width, width), fixed),
            pl.BlockSpec(color_head.shape, fixed),
        ],
        out_specs=[
            pl.BlockSpec((3, block_rows, LANES), lambda b: (0, b, 0)),
            pl.BlockSpec((block_rows, LANES), fixed),
            pl.BlockSpec((width, width), fixed),
            pl.BlockSpec((width, width), fixed),
        ],
        out_shape=[
            jax.ShapeDtypeStruct((3, rows, LANES), jnp.float32),
            jax.ShapeDtypeStruct((block_rows, LANES), jnp.float32),
            jax.ShapeDtypeStruct((width, width), jnp.bfloat16),
            jax.ShapeDtypeStruct((width, width), jnp.bfloat16),
        ],
        scratch_shapes=[
            pltpu.VMEM((width, width), jnp.bfloat16),
            pltpu.VMEM((width, width), jnp.bfloat16),
            pltpu.VMEM((48, width), jnp.float32),
            pltpu.VMEM((width, width), jnp.float32),
            pltpu.VMEM((4, block_rows, LANES), jnp.float32),
            pltpu.VMEM((4, block), jnp.float32),
        ],
    )(
        flat_points,
        spacing.reshape(rows, LANES),
        wide_target,
        wide_factor,
        w_first,
        w_second,
        color_head,
    )
    colors = color.reshape(3, slots, ray_depth)[:, :, 0]
    return colors, jnp.sum(loss) * (1.0 / ray_depth), grad_first, grad_second


MESH = pl.DeviceIdType.MESH


def greet_all(groups, shards):
    me = lax.axis_index("grp") * shards + lax.axis_index("shard")
    total = groups * shards
    barrier = pltpu.get_barrier_semaphore()

    def greet(step, carry):
        other = lax.rem(me + step, total)
        pl.semaphore_signal(
            barrier, inc=1, device_id=(other // shards, lax.rem(other, shards)), device_id_type=MESH
        )
        return carry

    lax.fori_loop(1, total, greet, 0)
    pl.semaphore_wait(barrier, total - 1)


def messages(groups, shards, message_ref, landed, sent, arrived):
    me = lax.axis_index("grp") * shards + lax.axis_index("shard")
    total = groups * shards

    def copy_to(step):
        other = lax.rem(me + step, total)
        return pltpu.make_async_remote_copy(
            src_ref=message_ref.at[other],
            dst_ref=landed.at[me],
            send_sem=sent.at[other],
            recv_sem=arrived.at[me],
            device_id=(other // shards, lax.rem(other, shards)),
            device_id_type=MESH,
        )

    def copy_from(step):
        other = lax.rem(me + total - step, total)
        return pltpu.make_async_remote_copy(
            src_ref=message_ref.at[other],
            dst_ref=landed.at[other],
            send_sem=sent.at[other],
            recv_sem=arrived.at[other],
            device_id=(other // shards, lax.rem(other, shards)),
            device_id_type=MESH,
        )

    def start():
        def one(step, carry):
            copy_to(step).start()
            return carry

        lax.fori_loop(1, total, one, 0)

    def finish():
        def one(step, carry):
            copy_from(step).wait_recv()
            copy_to(step).wait_send()
            return carry

        lax.fori_loop(1, total, one, 0)

    return start, finish


def tail_kernel(
    groups,
    shards,
    message_ref,
    turned_ref,
    field_ref,
    sums_ref,
    colors_ref,
    head_ref,
    landed,
    fields,
    part,
    parts,
    done,
    message_sent,
    message_arrived,
    field_sent,
    passed_on,
    field_arrived,
    part_sent,
    part_arrived,
    done_sent,
    done_arrived,
):
    group = lax.axis_index("grp")
    shard = lax.axis_index("shard")
    me = group * shards + shard
    chips = shards // 2
    chip = shard // 2
    core = lax.rem(shard, 2)
    partner = chip * 2 + 1 - core

    def remote(source, target, send_sem, recv_sem, to_group, to_shard):
        return pltpu.make_async_remote_copy(
            src_ref=source,
            dst_ref=target,
            send_sem=send_sem,
            recv_sem=recv_sem,
            device_id=(to_group, to_shard),
            device_id_type=MESH,
        )

    width = field_ref.shape[1] // HALVES

    def columns(half):
        return pl.ds(half * width, width)

    def field_to(half, other):
        return remote(
            field_ref.at[:, columns(half)],
            fields.at[half, shard],
            field_sent.at[half, other],
            field_arrived.at[half, shard],
            group,
            other,
        )

    def field_pass(half, origin):
        return remote(
            fields.at[half, origin],
            fields.at[half, origin],
            passed_on.at[half, origin],
            field_arrived.at[half, origin],
            group,
            partner,
        )

    greet_all(groups, shards)
    start_messages, finish_messages = messages(
        groups, shards, message_ref, landed, message_sent, message_arrived
    )
    peers = [lax.rem(chip + step, chips) * 2 + core for step in range(1, chips)]
    origins = [lax.rem(chip + chips - step, chips) * 2 + core for step in range(1, chips)]
    group_steps = [lax.rem(group + step, groups) for step in range(1, groups)]
    for half in range(HALVES):
        for other in peers:
            field_to(half, other).start()
        field_to(half, partner).start()
    start_messages()

    def product(rows, field):
        return jnp.dot(rows, field, preferred_element_type=jnp.float32)

    def part_to(half, other):
        return remote(
            part.at[half, other],
            parts.at[half, group],
            part_sent.at[half, other],
            part_arrived.at[half, group],
            other,
            shard,
        )

    def part_from(half, other):
        return remote(
            part.at[half, other],
            parts.at[half, other],
            part_sent.at[half, other],
            part_arrived.at[half, other],
            other,
            shard,
        )

    def done_to(half, other):
        return remote(
            done.at[half, group],
            done.at[half, group],
            done_sent.at[half, other],
            done_arrived.at[half, group],
            other,
            shard,
        )

    def done_from(half, other):
        return remote(
            done.at[half, other],
            done.at[half, other],
            done_sent.at[half, other],
            done_arrived.at[half, other],
            other,
            shard,
        )

    def gather_half(half):
        total = product(turned_ref[shard], field_ref[:, half * width : (half + 1) * width])
        field_pass(half, partner).wait_recv()
        total = total + product(turned_ref[partner], fields[half, partner])
        for origin in origins:
            field_pass(half, origin).wait_recv()
            field_pass(half, origin).start()
            total = total + product(turned_ref[origin], fields[half, origin])
        for origin in origins:
            across = origin + 1 - 2 * core
            field_pass(half, across).wait_recv()
            total = total + product(turned_ref[across], fields[half, across])
        part[half] = total.astype(jnp.bfloat16).reshape(part.shape[1:])
        for other in group_steps:
            part_to(half, other).start()

    def sum_half(half):
        slice_sum = part[half, group].astype(jnp.float32)
        for other in group_steps:
            part_from(half, other).wait_recv()
            slice_sum = slice_sum + parts[half, other].astype(jnp.float32)
        done[half, group] = slice_sum.astype(jnp.bfloat16)
        for other in group_steps:
            done_to(half, other).start()
        head_ref[group, :, half * width : (half + 1) * width] = slice_sum

    for half in range(HALVES):
        gather_half(half)
        if half > 0:
            sum_half(half - 1)
    sum_half(HALVES - 1)

    finish_messages()
    landed[me] = message_ref[me]
    colors_ref[...] = landed[:, landed.shape[1] - 8 :, :]
    sums_ref[...] = jnp.sum(landed[...], axis=0)

    for half in range(HALVES):
        for other in group_steps:
            done_from(half, other).wait_recv()
            head_ref[other, :, half * width : (half + 1) * width] = done[half, other].astype(
                jnp.float32
            )
        for other in peers:
            field_to(half, other).wait_send()
        field_to(half, partner).wait_send()
        for origin in origins:
            field_pass(half, origin).wait_send()
        for other in group_steps:
            part_to(half, other).wait_send()
            done_to(half, other).wait_send()


def tail_exchange(groups, shards, turned, d_field, gain_part, loss_sum, slot_colors):
    tokens, model = d_field.shape
    devices = groups * shards
    rows = model // shards
    gain_rows = model // LANES
    per_device = slot_colors.shape[1] // devices
    shared = jnp.concatenate(
        [gain_part.reshape(gain_rows, LANES), jnp.broadcast_to(loss_sum, (1, LANES))], axis=0
    )
    own = jnp.pad(
        slot_colors.reshape(3, devices, per_device).transpose(1, 0, 2),
        ((0, 0), (0, 4), (0, LANES - per_device)),
    )
    message = jnp.concatenate(
        [jnp.broadcast_to(shared[None], (devices,) + shared.shape), own], axis=1
    )
    in_vmem = pl.BlockSpec(memory_space=pltpu.VMEM)
    dma = pltpu.SemaphoreType.DMA
    sums, colors, head = pl.pallas_call(
        functools.partial(tail_kernel, groups, shards),
        in_specs=[in_vmem] * 3,
        out_specs=[in_vmem] * 3,
        out_shape=[
            jax.ShapeDtypeStruct(message.shape[1:], jnp.float32),
            jax.ShapeDtypeStruct((devices, 8, LANES), jnp.float32),
            jax.ShapeDtypeStruct((groups, rows // groups, model), jnp.float32),
        ],
        scratch_shapes=[
            pltpu.VMEM(message.shape, jnp.float32),
            pltpu.VMEM((HALVES, shards, tokens, model // HALVES), jnp.bfloat16),
            pltpu.VMEM((HALVES, groups, rows // groups, model // HALVES), jnp.bfloat16),
            pltpu.VMEM((HALVES, groups, rows // groups, model // HALVES), jnp.bfloat16),
            pltpu.VMEM((HALVES, groups, rows // groups, model // HALVES), jnp.bfloat16),
            dma((devices,)),
            dma((devices,)),
            dma((HALVES, shards)),
            dma((HALVES, shards)),
            dma((HALVES, shards)),
            dma((HALVES, groups)),
            dma((HALVES, groups)),
            dma((HALVES, groups)),
            dma((HALVES, groups)),
        ],
        compiler_params=pltpu.CompilerParams(collective_id=1, has_side_effects=True),
    )(message, turned, d_field)
    gain = sums[:gain_rows].reshape(model)
    loss = sums[gain_rows, 0]
    returned = colors[:, 1:4, :per_device].transpose(1, 0, 2).reshape(3, devices * per_device)
    return returned, loss, head.reshape(rows, model), gain


def start_kernel(
    groups,
    shards,
    message_ref,
    turned_ref,
    weight_ref,
    received_ref,
    turned_all_ref,
    weight_all_ref,
    field_ref,
    landed,
    turned,
    weights,
    message_sent,
    message_arrived,
    turned_sent,
    turned_arrived,
    weight_sent,
    passed_on,
    weight_arrived,
):
    group = lax.axis_index("grp")
    shard = lax.axis_index("shard")
    me = group * shards + shard
    chips = shards // 2
    chip = shard // 2
    core = lax.rem(shard, 2)
    partner = chip * 2 + 1 - core

    def remote(source, target, send_sem, recv_sem, to_shard):
        return pltpu.make_async_remote_copy(
            src_ref=source,
            dst_ref=target,
            send_sem=send_sem,
            recv_sem=recv_sem,
            device_id=(group, to_shard),
            device_id_type=MESH,
        )

    def weight_to(other):
        return remote(
            weight_ref, weights.at[shard], weight_sent.at[other], weight_arrived.at[shard], other
        )

    def weight_pass(origin):
        return remote(
            weights.at[origin],
            weights.at[origin],
            passed_on.at[origin],
            weight_arrived.at[origin],
            partner,
        )

    def turned_to(other):
        return remote(
            turned_ref.at[other],
            turned.at[shard],
            turned_sent.at[other],
            turned_arrived.at[shard],
            other,
        )

    def turned_from(other):
        return remote(
            turned_ref.at[other],
            turned.at[other],
            turned_sent.at[other],
            turned_arrived.at[other],
            other,
        )

    greet_all(groups, shards)
    start_messages, finish_messages = messages(
        groups, shards, message_ref, landed, message_sent, message_arrived
    )
    peers = [lax.rem(chip + step, chips) * 2 + core for step in range(1, chips)]
    origins = [lax.rem(chip + chips - step, chips) * 2 + core for step in range(1, chips)]
    others = [lax.rem(shard + step, shards) for step in range(1, shards)]
    for other in peers:
        weight_to(other).start()
    weight_to(partner).start()
    start_messages()
    for other in others:
        turned_to(other).start()

    def product(rows, weight):
        return lax.dot_general(
            rows, weight, (((0,), (0,)), ((), ())), preferred_element_type=jnp.float32
        )

    total = product(turned_ref[shard], weight_ref[...])
    weight_all_ref[shard] = weight_ref[...]
    turned_all_ref[shard] = turned_ref[shard]
    weight_pass(partner).wait_recv()
    total = total + product(turned_ref[partner], weights[partner])
    weight_all_ref[partner] = weights[partner]
    for origin in origins:
        weight_pass(origin).wait_recv()
        weight_pass(origin).start()
        total = total + product(turned_ref[origin], weights[origin])
        weight_all_ref[origin] = weights[origin]
    for origin in origins:
        across = origin + 1 - 2 * core
        weight_pass(across).wait_recv()
        total = total + product(turned_ref[across], weights[across])
        weight_all_ref[across] = weights[across]
    field_ref[...] = total.astype(jnp.bfloat16)

    finish_messages()
    landed[me] = message_ref[me]
    received_ref[...] = landed[...]
    for other in others:
        turned_from(other).wait_recv()
        turned_all_ref[other] = turned[other]
    for other in peers:
        weight_to(other).wait_send()
    weight_to(partner).wait_send()
    for origin in origins:
        weight_pass(origin).wait_send()
    for other in others:
        turned_to(other).wait_send()


def start_exchange(groups, shards, x_norm, head_weight, send):
    tokens, model = x_norm.shape
    devices = groups * shards
    rows = model // shards
    turned = x_norm.T.reshape(shards, rows, tokens)
    message = send.reshape(devices, send.shape[0] // devices, send.shape[1])
    in_vmem = pl.BlockSpec(memory_space=pltpu.VMEM)
    dma = pltpu.SemaphoreType.DMA
    received, turned_all, weight_all, field = pl.pallas_call(
        functools.partial(start_kernel, groups, shards),
        in_specs=[in_vmem] * 3,
        out_specs=[in_vmem] * 4,
        out_shape=[
            jax.ShapeDtypeStruct(message.shape, jnp.float32),
            jax.ShapeDtypeStruct(turned.shape, jnp.bfloat16),
            jax.ShapeDtypeStruct((shards, rows, model), jnp.bfloat16),
            jax.ShapeDtypeStruct((tokens, model), jnp.bfloat16),
        ],
        scratch_shapes=[
            pltpu.VMEM(message.shape, jnp.float32),
            pltpu.VMEM(turned.shape, jnp.bfloat16),
            pltpu.VMEM((shards, rows, model), jnp.bfloat16),
            dma((devices,)),
            dma((devices,)),
            dma((shards,)),
            dma((shards,)),
            dma((shards,)),
            dma((shards,)),
            dma((shards,)),
        ],
        compiler_params=pltpu.CompilerParams(collective_id=2, has_side_effects=True),
    )(message, turned, head_weight)
    return received.reshape(send.shape), turned_all, weight_all.reshape(model, model), field


def body(
    latents,
    head_weight,
    norm_gain,
    color_head,
    sample_points,
    sample_spacing,
    ray_targets,
    ray_scene,
):
    devices = lax.axis_size(("grp", "shard"))
    ray_count, ray_depth = sample_spacing.shape
    tokens, model = latents.shape
    field_width = color_head.shape[1]
    per_layer = field_width * field_width // model
    per_device = 4 * ray_count // devices
    slot_total = per_device * devices
    latent_f32 = latents.astype(jnp.float32)
    inv_rms = lax.rsqrt(jnp.mean(latent_f32 * latent_f32, axis=1, keepdims=True) + norm_eps)
    x_hat = latent_f32 * inv_rms
    x_norm = (x_hat * norm_gain).astype(jnp.bfloat16)
    ray_ids = jnp.arange(ray_count, dtype=jnp.int32)
    same_scene = ray_scene[:, None] == ray_scene[None, :]
    earlier = ray_ids[:, None] < ray_ids[None, :]
    ray_rank = jnp.sum(jnp.logical_and(same_scene, earlier).astype(jnp.int32), axis=0)
    slot_of_ray = ray_scene * per_device + ray_rank
    payload = jnp.concatenate(
        [sample_points, sample_spacing, ray_targets.T, jnp.ones((ray_count, 1), jnp.float32)], axis=1
    )
    send = jnp.zeros((slot_total, payload.shape[1]), jnp.float32).at[slot_of_ray].set(payload)
    received, x_turned, full_weight, field_rows = start_exchange(
        lax.axis_size("grp"), lax.axis_size("shard"), x_norm, head_weight, send
    )
    w_first = field_rows[:per_layer].reshape(field_width, field_width)
    w_second = field_rows[per_layer:].reshape(field_width, field_width)
    recv_points = received[:, : 3 * ray_depth]
    recv_spacing = received[:, 3 * ray_depth : 4 * ray_depth]
    recv_target = received[:, 4 * ray_depth : 4 * ray_depth + 3]
    recv_live = received[:, 4 * ray_depth + 3]
    scene_rays = jnp.sum(recv_live)
    scene_factor = 1.0 / (devices * scene_rays)

    slot_colors, loss_sum, grad_first, grad_second = render_slots(
        recv_points,
        recv_spacing,
        recv_target,
        recv_live * scene_factor,
        w_first,
        w_second,
        color_head,
    )
    d_field = jnp.concatenate(
        [grad_first.reshape(per_layer, model), grad_second.reshape(per_layer, model)], axis=0
    )
    d_norm = lax.dot_general(
        d_field,
        full_weight,
        (((1,), (1,)), ((), ())),
        preferred_element_type=jnp.float32,
    )
    gain_part = jnp.sum(d_norm * x_hat, axis=0)
    returned, loss_total, head_grad, norm_gain_grad = tail_exchange(
        lax.axis_size("grp"), lax.axis_size("shard"), x_turned, d_field, gain_part, loss_sum, slot_colors
    )
    rendered = returned[:, slot_of_ray]
    d_scaled = d_norm * norm_gain
    latent_grad = (
        inv_rms * (d_scaled - x_hat * jnp.mean(d_scaled * x_hat, axis=1, keepdims=True))
    ).astype(jnp.bfloat16)
    return (rendered, loss_total, head_grad, norm_gain_grad, latent_grad)


def solution(mesh):
    placed = (
        P(("grp", "shard"), None),
        P("shard", None),
        P(),
        P(),
        P(("grp", "shard"), None),
        P(("grp", "shard"), None),
        P(None, ("grp", "shard")),
        P(("grp", "shard")),
    )
    return jax.shard_map(
        body,
        mesh=mesh,
        in_specs=placed,
        out_specs=(
            P(None, ("grp", "shard")),
            P(),
            P("shard", None),
            P(),
            P(("grp", "shard"), None),
        ),
        check_vma=False,
    )
```

profile of v0, /device:TPU:0, one launch (start us, length us, event | category | flops | bytes accessed | tf_op | source)
XLA Modules:
  0.0 124.1 jit_solution(14302594915065280813)
XLA Ops:
  0.6 0.8 convert_reduce_fusion
  2.1 1.1 fusion.10
  3.3 0.8 copy.30
  4.1 1.1 fusion.11
  5.2 0.8 copy.31
  6.0 1.9 %scatter_custom_fusion = f32[256,260]{1,0:T(8,128)} fusion(s32[64]{0:T(128)S(1)} %compare_select_fusion, f32[]{:T(128)} %constant.9.clone.1, f32[64,3]{1,0:T(8,128)S(1)} %copy.30, f32[]{:T(128)} %constant.31, f32[64,64]{1,0:T(8,128)} %param.13, f32[64,192]{1,0:T(8,128)} %param.12, f32[260]{0:T(512)S(1)} %pad.11.clone), kind=kCustom, calls=%fused_computation.19 | custom fusion | flops 49920 | bytes 366600 | tf_op jit(solution)/shard_map/scatter | solution.py:681
  7.9 30.7 %shard_map.119 = (f32[32,8,260]{2,1,0:T(8,128)}, bf16[8,128,128]{2,1,0:T(8,128)(2,1)}, bf16[8,128,1024]{2,1,0:T(8,128)(2,1)}, bf16[128,1024]{1,0:T(8,128)(2,1)}) custom-call(f32[32,8,260]{2,1,0:T(8,128)} %bitcast.30, bf16[8,128,128]{2,1,0:T(8,128)(2,1)} %bitcast.35, bf16[128,1024]{1,0:T(8,128)(2,1)} %weight_ref.1), custom_call_target="tpu_custom_call" | custom-call | tf_op jit(solution)/shard_map/pallas_call | solution.py:625
  38.7 1.0 slice_bitcast_fusion
  39.7 1.0 slice.43
  41.4 1.6 %slice_reduce_fusion.1 = (f32[]{:T(128)}, f32[256,1]{1,0:T(8,128)S(1)}) fusion(f32[256,260]{1,0:T(8,128)} %bitcast.33), kind=kLoop, calls=%fused_computation.42 | loop fusion | flops 255 | bytes 2052 | tf_op jit(solution)/shard_map/reduce_sum | solution.py:691
  43.7 1.0 slice.42
  46.1 0.9 reshape.86.points_ref
  48.7 0.8 reshape.88.target_ref
  49.5 29.1 %shard_map.120 = (f32[3,128,128]{2,1,0:T(8,128)}, f32[16,128]{1,0:T(8,128)}, bf16[256,256]{1,0:T(8,128)(2,1)}, bf16[256,256]{1,0:T(8,128)(2,1)}) custom-call(f32[3,16384]{1,0:T(4,128)} %reshape.86.points_ref, f32[128,128]{1,0:T(8,128)} %reshape.87.spacing_ref, f32[3,128,128]{2,1,0:T(8,128)} %reshape.88.target_ref, f32[128,128]{1,0:T(8,128)} %copy.37.factor_ref, ...), custom_call_target="tpu_custom_call" | custom-call | tf_op jit(solution)/shard_map/pallas_call | solution.py:159
  78.6 1.3 %reduce_sum.58 = f32[]{:T(128)} reduce(f32[16,128]{1,0:T(8,128)} %get-tuple-element.21, f32[]{:T(128)} %constant.9.clone.1), dimensions={0,1}, to_apply=%region_5.0 | reduce | flops 2047 | bytes 8200 | tf_op jit(solution)/shard_map/reduce_sum | solution.py:201
  80.5 1.0 reshape.91
  81.6 1.0 reshape.92
  82.6 0.9 fusion.6
  83.6 0.9 fusion.9
  85.7 31.6 %shard_map.121 = (f32[16,128]{1,0:T(8,128)}, f32[32,8,128]{2,1,0:T(8,128)}, f32[4,32,1024]{2,1,0:T(8,128)}) custom-call(f32[32,16,128]{2,1,0:T(8,128)} %select_maximum_fusion.message_ref, bf16[8,128,128]{2,1,0:T(8,128)(2,1)} %get-tuple-element.23.turned_ref, bf16[128,1024]{1,0:T(8,128)(2,1)} %copy-done.2), custom_call_target="tpu_custom_call" | custom-call | tf_op jit(solution)/shard_map/pallas_call | solution.py:461
  117.4 1.2 slice.38
  118.5 0.9 slice_bitcast_fusion.1
  119.5 1.3 %slice_bitcast_fusion.2 = f32[1024]{0:T(1024)} fusion(f32[16,128]{1,0:T(8,128)} %get-tuple-element.25), kind=kLoop, calls=%fused_computation.37 | loop fusion | bytes 8192 | tf_op jit(solution)/shard_map/reshape | solution.py:488
  122.2 1.9 %copy.51 = f32[128,1024]{1,0:T(8,128)} copy(f32[128,1024]{1,0:T(8,128)} %bitcast.37) | data formatting | bytes 1048576
  (43 shorter events, 7.3 us)
Async XLA Ops:
  38.7 8.3 %copy-start.3 = (bf16[128,1024]{1,0:T(8,128)(2,1)S(1)}, bf16[128,1024]{1,0:T(8,128)(2,1)}, u32[]{:S(2)}) copy-start(bf16[128,1024]{1,0:T(8,128)(2,1)} %get-tuple-element.17) | copy-start | bytes 786436
  47.0 35.6 %copy-start = (bf16[128,1024]{1,0:T(8,128)(2,1)S(1)}, bf16[128,1024]{1,0:T(8,128)(2,1)}, u32[]{:S(2)}) copy-start(bf16[128,1024]{1,0:T(8,128)(2,1)} %param.8) | copy-start | bytes 786436
  47.0 35.6 %copy-start.1 = (bf16[8,128,1024]{2,1,0:T(8,128)(2,1)S(1)}, bf16[8,128,1024]{2,1,0:T(8,128)(2,1)}, u32[]{:S(2)}) copy-start(bf16[8,128,1024]{2,1,0:T(8,128)(2,1)} %get-tuple-element.20) | copy-start | bytes 6291460
  47.0 35.6 %copy-start.5 = (f32[1024]{0:T(1024)S(1)}, f32[1024]{0:T(1024)}, u32[]{:S(2)}) copy-start(f32[1024]{0:T(1024)} %param.10) | copy-start | bytes 12292
  82.6 1.9 %copy-start.2 = (bf16[128,1024]{1,0:T(8,128)(2,1)}, bf16[128,1024]{1,0:T(8,128)(2,1)S(1)}, u32[]{:S(2)}) copy-start(bf16[128,1024]{1,0:T(8,128)(2,1)S(1)} %constant_dynamic-update-slice_fusion.field_ref) | copy-start | bytes 786436
  82.6 1.9 %copy-start.4 = (f32[3,128,128]{2,1,0:T(8,128)S(1)}, f32[3,128,128]{2,1,0:T(8,128)}, u32[]{:S(2)}) copy-start(f32[3,128,128]{2,1,0:T(8,128)} %get-tuple-element.22) | copy-start | bytes 589828
where the time goes:
time: 125 us; the launch traced here: 124 us
  Pallas kernels  91.5 us (73%)
  local copies, waits for them, and re-layouts  19.3 us (15%)
  other arithmetic  10.2 us (8%)
  between operations  2.17 us (2%)
    pallas_call x1, Pallas kernels, tail_exchange(): pl.pallas_call(functools.partial(tail_kernel, groups, shards), in_specs=[...  31.6 us
    pallas_call x1, Pallas kernels, start_exchange(): pl.pallas_call(functools.partial(start_kernel, groups, shards), in_specs=...  30.7 us
    pallas_call x1, Pallas kernels, render_slots(): pl.pallas_call(functools.partial(ray_kernel, ray_depth), grid=(total // b...  29.1 us
    unnamed x17, local copies, waits for them, and re-layouts  2.76 us

commit v1 on v0

v1 whole, which is shorter than its diff:
```python
import functools

import jax
import jax.numpy as jnp
from jax import lax
from jax.experimental import pallas as pl
from jax.experimental.pallas import tpu as pltpu
from jax.sharding import PartitionSpec as P

norm_eps = 1e-06

LANES = 128
HALVES = 2
FEATURES = 48
FOLDED = 16
BLOCK = 1024
SINE = (3.14159265358979, -5.16771278004997, 2.55016403987735, -0.599264529320792, 0.0821458866111282, -0.00737043094571435, 0.000466302805767613, -0.0000219153534478303)
MESH = pl.DeviceIdType.MESH


def sine_of_pi(turns):
    whole = jnp.floor(turns + 0.5)
    rest = turns - whole
    odd = whole - 2.0 * jnp.floor(whole * 0.5)
    square = rest * rest
    value = jnp.full_like(square, SINE[-1])
    for coefficient in SINE[-2::-1]:
        value = value * square + coefficient
    return value * (rest * (1.0 - 2.0 * odd))


def product(a, b):
    return jnp.dot(a, b, preferred_element_type=jnp.float32)


def exact(a, b, contract=(1, 0)):
    return lax.dot_general(
        a,
        b,
        (((contract[0],), (contract[1],)), ((), ())),
        preferred_element_type=jnp.float32,
        precision=lax.Precision.HIGHEST,
    )


def over_first(a, b):
    return lax.dot_general(a, b, (((0,), (0,)), ((), ())), preferred_element_type=jnp.float32)


def over_last(a, b):
    return lax.dot_general(a, b, (((1,), (1,)), ((), ())), preferred_element_type=jnp.float32)


def iota(shape, axis):
    return lax.broadcasted_iota(jnp.int32, shape, axis)


def store_rows(ref, start, count, stride, values):
    for lanes in range(ref.shape[0]):
        ref[lanes, pl.ds(start, count, stride=stride), :] = values[:, lanes * LANES : (lanes + 1) * LANES]


def load_rows(ref, start, count, stride):
    return jnp.concatenate(
        [ref[lanes, pl.ds(start, count, stride=stride), :] for lanes in range(ref.shape[0])], axis=1
    )


def joined(ref):
    return jnp.concatenate([ref[lanes] for lanes in range(ref.shape[0])], axis=1)


def encode_rows(axes, encoded):
    sines = [sine_of_pi(a) for a in axes]
    cosines = [sine_of_pi(a + 0.5) for a in axes]
    octaves = FEATURES // 6
    for octave in range(octaves):
        for c in range(3):
            encoded[pl.ds(octave * 6 + c, 8, stride=FEATURES), :] = sines[c]
            encoded[pl.ds(octave * 6 + 3 + c, 8, stride=FEATURES), :] = cosines[c]
        if octave < octaves - 1:
            for c in range(3):
                twice = sines[c] + sines[c]
                sines[c], cosines[c] = twice * cosines[c], 1.0 - twice * sines[c]


def forward_block(i, coords, first, second_t, head, encoded, zeros_all, ones_all, twos_all, raw):
    row = pl.multiple_of(i * 8, 8)
    encode_rows([coords[c, pl.ds(row, 8), :] for c in range(3)], encoded)
    h_zero = jnp.concatenate(
        [encoded[FEATURES * r : FEATURES * (r + 1), :].astype(jnp.bfloat16) for r in range(8)], axis=1
    )
    at = pl.multiple_of(i * BLOCK, BLOCK)
    zeros_all[:, pl.ds(at, BLOCK)] = h_zero
    twice = jnp.concatenate([h_zero, h_zero], axis=0)
    h_one = jnp.maximum(product(first[...], twice).astype(jnp.bfloat16), 0)
    ones_all[:, pl.ds(at, BLOCK)] = h_one
    h_two = jnp.maximum(product(second_t[...], h_one).astype(jnp.bfloat16), 0)
    twos_all[:, pl.ds(at, BLOCK)] = h_two
    values = product(head[...], h_two)
    for r in range(8):
        for c in range(4):
            raw[c, pl.ds(row + r, 1), :] = values[c : c + 1, r * LANES : (r + 1) * LANES]


def backward_block(i, draw, second, head_t, zeros_all, ones_all, twos_all, grad_first, grad_second):
    at = pl.multiple_of(i * BLOCK, BLOCK)
    d_raw = draw[:, pl.ds(at, BLOCK)].astype(jnp.bfloat16)
    zero = jnp.zeros((), jnp.bfloat16)
    d_two = product(head_t[...], d_raw).astype(jnp.bfloat16)
    d_atwo = jnp.where(twos_all[:, pl.ds(at, BLOCK)] > 0, d_two, zero)
    h_one = ones_all[:, pl.ds(at, BLOCK)]
    grad_second[...] += over_last(h_one, d_atwo)
    d_one = product(second[...], d_atwo).astype(jnp.bfloat16)
    d_aone = jnp.where(h_one > 0, d_one, zero)
    grad_first[...] += over_last(zeros_all[:, pl.ds(at, BLOCK)], d_aone)


def render_middle(ray_depth, raw, spacing, targets, factor, draw):
    row = iota((LANES, LANES), 0)
    column = iota((LANES, LANES), 1)
    same = row // ray_depth == column // ray_depth
    before_sum = jnp.where(jnp.logical_and(same, row < column), 1.0, 0.0)
    behind_sum = jnp.where(jnp.logical_and(same, row > column), 1.0, 0.0)
    whole_sum = jnp.where(same, 1.0, 0.0)
    density_raw = raw[0]
    density = jnp.maximum(density_raw, 0.0) + jnp.log1p(jnp.exp(-jnp.abs(density_raw)))
    optical = density * spacing
    transmit = jnp.exp(-exact(optical, before_sum))
    survive = jnp.exp(-optical)
    blend = transmit * (1.0 - survive)
    d_blend = jnp.zeros_like(blend)
    loss = jnp.zeros_like(blend)
    tints = []
    colors = []
    for c in range(3):
        albedo = 1.0 / (1.0 + jnp.exp(-raw[c + 1]))
        color = exact(blend * (albedo - 1.0), whole_sum) + 1.0
        colors.append(color)
        residual = color - targets[c]
        loss = loss + residual * residual
        grad_color = 2.0 * residual * factor
        d_blend = d_blend + grad_color * (albedo - 1.0)
        tints.append(grad_color * blend * albedo * (1.0 - albedo))
    behind = exact(d_blend * blend, behind_sum)
    d_optical = d_blend * transmit * survive - behind
    d_density = d_optical * spacing * (1.0 / (1.0 + jnp.exp(-density_raw)))
    for c, value in enumerate([d_density] + tints):
        for i in range(value.shape[0]):
            draw[c : c + 1, i * LANES : (i + 1) * LANES] = value[i : i + 1, :]
    return colors, loss * factor


def greet_all(groups, shards):
    me = lax.axis_index("grp") * shards + lax.axis_index("shard")
    total = groups * shards
    barrier = pltpu.get_barrier_semaphore()

    def greet(step, carry):
        other = lax.rem(me + step, total)
        pl.semaphore_signal(
            barrier, inc=1, device_id=(other // shards, lax.rem(other, shards)), device_id_type=MESH
        )
        return carry

    lax.fori_loop(1, total, greet, 0)
    return lambda: pl.semaphore_wait(barrier, total - 1)


def messages(groups, shards, source, landed, sent, arrived):
    me = lax.axis_index("grp") * shards + lax.axis_index("shard")
    total = groups * shards

    def copy(other, place):
        return pltpu.make_async_remote_copy(
            src_ref=source(other),
            dst_ref=landed.at[place],
            send_sem=sent.at[other],
            recv_sem=arrived.at[place],
            device_id=(other // shards, lax.rem(other, shards)),
            device_id_type=MESH,
        )

    def start():
        def one(step, carry):
            copy(lax.rem(me + step, total), me).start()
            return carry

        lax.fori_loop(1, total, one, 0)

    def receive():
        def one(step, carry):
            other = lax.rem(me + total - step, total)
            copy(other, other).wait_recv()
            return carry

        lax.fori_loop(1, total, one, 0)

    def finish():
        def one(step, carry):
            copy(lax.rem(me + step, total), me).wait_send()
            return carry

        lax.fori_loop(1, total, one, 0)

    return start, receive, finish


def plane_gather(source, place, sent, passed, arrived):
    group = lax.axis_index("grp")
    shard = lax.axis_index("shard")
    shards = lax.axis_size("shard")
    chips = shards // 2
    chip = shard // 2
    core = lax.rem(shard, 2)
    partner = chip * 2 + 1 - core
    peers = [lax.rem(chip + step, chips) * 2 + core for step in range(1, chips)]
    origins = [lax.rem(chip + chips - step, chips) * 2 + core for step in range(1, chips)]

    def remote(src, dst, send_sem, recv_sem, to):
        return pltpu.make_async_remote_copy(
            src_ref=src,
            dst_ref=dst,
            send_sem=send_sem,
            recv_sem=recv_sem,
            device_id=(group, to),
            device_id_type=MESH,
        )

    def to(other):
        return remote(source, place(shard), sent.at[other], arrived.at[shard], other)

    def passing(origin):
        return remote(place(origin), place(origin), passed.at[origin], arrived.at[origin], partner)

    def start():
        for other in peers:
            to(other).start()
        to(partner).start()

    def receive(use):
        passing(partner).wait_recv()
        use(partner)
        for origin in origins:
            passing(origin).wait_recv()
            passing(origin).start()
            use(origin)
        for origin in origins:
            across = origin + 1 - 2 * core
            passing(across).wait_recv()
            use(across)

    def finish():
        for other in peers:
            to(other).wait_send()
        to(partner).wait_send()
        for origin in origins:
            passing(origin).wait_send()

    return start, receive, finish


def whole_kernel(
    groups,
    shards,
    latent_ref,
    weight_ref,
    weight_part_ref,
    gain_ref,
    gain_rows_ref,
    head_ref,
    points_ref,
    spacing_ref,
    target_ref,
    scene_ref,
    color_ref,
    loss_ref,
    grad_ref,
    gain_grad_ref,
    latent_grad_ref,
    message,
    landed,
    turned_own,
    turned,
    weights,
    wide_first,
    wide_second,
    first_t,
    second,
    second_t,
    head_t,
    encoded,
    coords,
    zeros_all,
    ones_all,
    twos_all,
    raw,
    draw,
    grad_first,
    grad_second,
    shades,
    landed_shades,
    d_field,
    fields,
    part,
    parts,
    done,
    gain_row,
    landed_gain,
    message_sent,
    message_arrived,
    shade_sent,
    shade_arrived,
    gain_sent,
    gain_arrived,
    turned_sent,
    turned_arrived,
    weight_sent,
    weight_passed,
    weight_arrived,
    field_sent,
    field_passed,
    field_arrived,
    part_sent,
    part_arrived,
    done_sent,
    done_arrived,
):
    group = lax.axis_index("grp")
    shard = lax.axis_index("shard")
    me = group * shards + shard
    total = groups * shards
    tokens, model = latent_ref.shape
    rows = model // shards
    width = head_ref.shape[1]
    ray_count, ray_depth = spacing_ref.shape
    slots = 4 * ray_count // total
    pairs = slots // 2
    fan_scale = width ** (-0.5)
    per_layer = width * width // model
    strips = model // width
    period = FEATURES // strips
    fold_rows = 2 * FOLDED + per_layer
    sent_rows = FOLDED + per_layer
    f32 = jnp.float32
    bf16 = jnp.bfloat16

    wait_all = greet_all(groups, shards)

    latent = latent_ref[...].astype(f32)
    inv_rms = lax.rsqrt(jnp.mean(latent * latent, axis=1, keepdims=True) + norm_eps)
    x_norm = (latent * inv_rms * gain_ref[...]).astype(bf16)
    fold = jnp.where(
        iota((FOLDED, per_layer), 1) % period == iota((FOLDED, per_layer), 0), 1.0, 0.0
    ).astype(bf16)
    folded = product(fold, x_norm[:per_layer])
    folded_high = folded.astype(bf16).astype(f32)
    stacked = jnp.concatenate(
        [folded_high, folded - folded_high, x_norm[per_layer:].astype(f32)], axis=0
    )
    turned_own[...] = stacked.T.astype(bf16).reshape(turned_own.shape)

    scene = scene_ref[...]
    ray_row = iota((ray_count, ray_count), 0)
    ray_column = iota((ray_count, ray_count), 1)
    scene_wide = jnp.broadcast_to(scene, (ray_count, ray_count))
    scene_tall = jnp.sum(jnp.where(ray_row == ray_column, scene_wide, 0), axis=1, keepdims=True)
    same_scene = scene_tall == scene_wide
    rank_wide = jnp.sum(
        jnp.where(jnp.logical_and(same_scene, ray_row < ray_column), 1, 0), axis=0, keepdims=True
    )
    rank_tall = jnp.sum(
        jnp.where(jnp.logical_and(same_scene, ray_column < ray_row), 1, 0), axis=1, keepdims=True
    )
    plane_axes = points_ref[:, :LANES]
    depth_axes = jnp.concatenate([points_ref[:, LANES:], spacing_ref[...]], axis=1)
    owner = iota((total, ray_count), 0)
    mine = scene == owner
    lane = iota((1, LANES), 1)
    for j in range(slots):
        chosen = jnp.where(jnp.logical_and(mine, rank_wide == j), 1.0, 0.0)
        message[:, j, :] = exact(chosen, plane_axes)
        message[:, slots + j, :] = exact(chosen, depth_axes)
    spread = jnp.where(iota((3, LANES), 1) // slots == iota((3, LANES), 0), 1.0, 0.0)
    extra = exact(target_ref[...], spread, (0, 0)) + jnp.where(lane // slots == 3, 1.0, 0.0)
    extra = jnp.where(rank_tall == lane % slots, extra, 0.0)
    message[:, 2 * slots, :] = exact(jnp.where(mine, 1.0, 0.0), extra)
    head_t[...] = (head_ref[...].astype(f32) * fan_scale).T.astype(bf16)
    grad_first[...] = jnp.zeros_like(grad_first)
    grad_second[...] = jnp.zeros_like(grad_second)

    wait_all()

    def weight_place(origin):
        return weights.at[pl.ds(pl.multiple_of(origin * rows, rows), rows)]

    def weight_of(origin):
        return weights[pl.ds(pl.multiple_of(origin * rows, rows), rows), :]

    start_weights, receive_weights, finish_weights = plane_gather(
        weight_ref, weight_place, weight_sent, weight_passed, weight_arrived
    )
    start_messages, receive_messages, finish_messages = messages(
        groups, shards, lambda other: message.at[other], landed, message_sent, message_arrived
    )
    start_weights()
    start_messages()
    weights[pl.ds(pl.multiple_of(shard * rows, rows), rows), :] = weight_ref[...]
    landed[me] = message[me]
    field_sum = [over_first(turned_own[shard], weight_ref[...])]

    def add_field(origin):
        field_sum[0] = field_sum[0] + over_first(turned_own[origin], weight_of(origin))

    receive_weights(add_field)

    def turned_copy(other, place):
        return pltpu.make_async_remote_copy(
            src_ref=turned_own.at[other],
            dst_ref=turned.at[place],
            send_sem=turned_sent.at[other],
            recv_sem=turned_arrived.at[place],
            device_id=(group, other),
            device_id_type=MESH,
        )

    others = [lax.rem(shard + step, shards) for step in range(1, shards)]
    for other in others:
        turned_copy(other, shard).start()
    turned[shard] = turned_own[shard]

    field = field_sum[0]
    first_rows = (field[:FOLDED] + field[FOLDED : 2 * FOLDED]) * fan_scale
    second_rows = field[2 * FOLDED :].astype(bf16).astype(f32) * fan_scale
    for m in range(strips):
        strip = slice(m * width, (m + 1) * width)
        store_rows(wide_first, m, FOLDED, strips, first_rows[:, strip])
        store_rows(wide_second, m, per_layer, strips, second_rows[:, strip])
    first = joined(wide_first)[:FEATURES]
    wide = joined(wide_second)
    first_high = first.astype(bf16).astype(f32)
    first_t[...] = jnp.concatenate([first_high, first - first_high], axis=0).T.astype(bf16)
    second[...] = wide.astype(bf16)
    second_t[...] = wide.T.astype(bf16)

    receive_messages()
    flat = jnp.concatenate([landed[:, j, :] for j in range(slots)], axis=0)
    deep = jnp.concatenate([landed[:, slots + j, :] for j in range(slots)], axis=0)
    extras = landed[:, 2 * slots, :]
    half_rows = pairs * total
    low = lane < ray_depth

    def unpack(values):
        lower, upper = values[:half_rows], values[half_rows:]
        return (
            jnp.where(low, lower, pltpu.roll(upper, ray_depth, 1)),
            jnp.where(low, pltpu.roll(lower, ray_depth, 1), upper),
        )

    coords[0], coords[1] = unpack(flat)
    coords[2], spacing = unpack(deep)

    def widen(c):
        return jnp.concatenate(
            [
                jnp.where(
                    low,
                    extras[:, c * slots + j : c * slots + j + 1],
                    extras[:, c * slots + j + pairs : c * slots + j + pairs + 1],
                )
                for j in range(pairs)
            ],
            axis=0,
        )

    scene_rays = jnp.sum(
        jnp.where(lane // slots == 3, extras, 0.0), axis=(0, 1), keepdims=True
    )
    factor = widen(3) / (total * scene_rays)
    targets = [widen(c) for c in range(3)]
    blocks = half_rows * LANES // BLOCK

    def forward(i, carry):
        forward_block(
            i, coords, first_t, second_t, head_ref, encoded, zeros_all, ones_all, twos_all, raw
        )
        return carry

    lax.fori_loop(0, blocks, forward, 0)
    colors, losses = render_middle(ray_depth, raw, spacing, targets, factor, draw)
    shade = jnp.where(
        lane == 3 * slots, jnp.sum(losses, axis=(0, 1), keepdims=True) * (1.0 / ray_depth), 0.0
    )
    shade = jnp.broadcast_to(shade, (total, LANES))
    for c in range(3):
        for j in range(pairs):
            values = colors[c][j * total : (j + 1) * total]
            at = c * slots + j
            shade = jnp.where(lane == at, values[:, 0:1], shade)
            shade = jnp.where(lane == at + pairs, values[:, ray_depth : ray_depth + 1], shade)
    shades[:, 0, :] = shade
    start_shades, receive_shades, finish_shades = messages(
        groups, shards, lambda other: shades.at[other], landed_shades, shade_sent, shade_arrived
    )
    start_shades()
    landed_shades[me] = shades[me]

    def backward(i, carry):
        backward_block(
            i, draw, second, head_t, zeros_all, ones_all, twos_all, grad_first, grad_second
        )
        return carry

    lax.fori_loop(0, blocks, backward, 0)

    for lanes in range(width // LANES):
        wide_first[lanes, :FEATURES, :] = grad_first[:, lanes * LANES : (lanes + 1) * LANES]
        wide_second[lanes] = grad_second[:, lanes * LANES : (lanes + 1) * LANES]
    columns = model // HALVES
    for m in range(strips):
        half, place = divmod(m * width, columns)
        strip = slice(place, place + width)
        head_rows = load_rows(wide_first, m, FOLDED, strips)
        head_rows = jnp.where(iota((FOLDED, 1), 0) < period, head_rows, 0.0)
        d_field[half, :FOLDED, strip] = head_rows.astype(bf16)
        d_field[half, FOLDED:, strip] = load_rows(wide_second, m, per_layer, strips).astype(bf16)

    gathers = [
        plane_gather(
            d_field.at[half],
            lambda origin, half=half: fields.at[half, origin],
            field_sent.at[half],
            field_passed.at[half],
            field_arrived.at[half],
        )
        for half in range(HALVES)
    ]
    for half in range(HALVES):
        gathers[half][0]()

    for other in others:
        turned_copy(other, other).wait_recv()

    group_steps = [lax.rem(group + step, groups) for step in range(1, groups)]

    def part_copy(half, other, place):
        return pltpu.make_async_remote_copy(
            src_ref=part.at[half, other],
            dst_ref=parts.at[half, place],
            send_sem=part_sent.at[half, other],
            recv_sem=part_arrived.at[half, place],
            device_id=(other, shard),
            device_id_type=MESH,
        )

    def done_copy(half, other, place):
        return pltpu.make_async_remote_copy(
            src_ref=done.at[half, place],
            dst_ref=done.at[half, place],
            send_sem=done_sent.at[half, other],
            recv_sem=done_arrived.at[half, place],
            device_id=(other, shard),
            device_id_type=MESH,
        )

    def head_term(origin, values):
        lead = values[:FOLDED]
        return product(turned[origin], jnp.concatenate([lead, lead, values[FOLDED:]], axis=0))

    def gather_half(half):
        head_sum = [head_term(shard, d_field[half])]

        def add_head(origin):
            head_sum[0] = head_sum[0] + head_term(origin, fields[half, origin])

        gathers[half][1](add_head)
        part[half] = head_sum[0].astype(bf16).reshape(part.shape[1:])
        for other in group_steps:
            part_copy(half, other, group).start()

    gain_terms = []

    def sum_half(half):
        slice_sum = part[half, group].astype(f32)
        for other in group_steps:
            part_copy(half, other, other).wait_recv()
            slice_sum = slice_sum + parts[half, other].astype(f32)
        done[half, group] = slice_sum.astype(bf16)
        for other in group_steps:
            done_copy(half, other, group).start()
        weight = weight_part_ref[group][:, half * columns : (half + 1) * columns].astype(f32)
        gain_terms.append(exact(jnp.ones((8, columns), f32), slice_sum * weight, (1, 1)))

    gather_half(0)
    gather_half(1)
    sum_half(0)
    sum_half(1)
    slice_rows = rows // groups
    gain_row[0:1, :slice_rows] = (gain_terms[0] + gain_terms[1])[0:1]
    start_gain, receive_gain, finish_gain = messages(
        groups, shards, lambda other: gain_row, landed_gain, gain_sent, gain_arrived
    )
    start_gain()
    landed_gain[me] = gain_row[...]

    token = iota((tokens, sent_rows), 0)
    source = jnp.where(token < per_layer, token % period, token - per_layer + FOLDED)
    copies = jnp.where(source == iota((tokens, sent_rows), 1), 1.0, 0.0).astype(bf16)
    own_field = jnp.concatenate([d_field[half] for half in range(HALVES)], axis=1)
    d_norm = over_last(product(copies, own_field).astype(bf16), weights[...])
    latent = latent_ref[...].astype(f32)
    inv_rms = lax.rsqrt(jnp.mean(latent * latent, axis=1, keepdims=True) + norm_eps)
    x_hat = latent * inv_rms
    d_scaled = d_norm * gain_ref[...]
    latent_grad_ref[...] = (
        inv_rms * (d_scaled - x_hat * jnp.mean(d_scaled * x_hat, axis=1, keepdims=True))
    ).astype(bf16)

    receive_shades()
    returned = landed_shades[:, 0, :]
    loss_ref[...] = jnp.sum(
        jnp.where(lane == 3 * slots, returned, 0.0), axis=(0, 1), keepdims=True
    )
    picked = exact(returned, jnp.where(mine, 1.0, 0.0), (0, 0))
    place = iota((LANES, ray_count), 0)
    for c in range(3):
        color_ref[c : c + 1, :] = jnp.sum(
            jnp.where(place == c * slots + rank_wide, picked, 0.0), axis=0, keepdims=True
        )

    for half in range(HALVES):
        grad_ref[group, :, half * columns : (half + 1) * columns] = done[half, group]
        for other in group_steps:
            done_copy(half, other, other).wait_recv()
            grad_ref[other, :, half * columns : (half + 1) * columns] = done[half, other]
    receive_gain()
    gains = landed_gain[:, 0, :slice_rows]
    gains = jnp.concatenate([gains[g * shards : (g + 1) * shards] for g in range(groups)], axis=1)
    gain_grad_ref[...] = gains / gain_rows_ref[...]

    finish_weights()
    finish_messages()
    finish_shades()
    finish_gain()
    for other in others:
        turned_copy(other, shard).wait_send()
    for half in range(HALVES):
        gathers[half][2]()
        for other in group_steps:
            part_copy(half, other, group).wait_send()
            done_copy(half, other, group).wait_send()


def body(
    latents,
    head_weight,
    norm_gain,
    color_head,
    sample_points,
    sample_spacing,
    ray_targets,
    ray_scene,
):
    groups, shards = lax.axis_size("grp"), lax.axis_size("shard")
    devices = groups * shards
    ray_count, ray_depth = sample_spacing.shape
    tokens, model = latents.shape
    width = color_head.shape[1]
    rows = model // shards
    slots = 4 * ray_count // devices
    per_layer = width * width // model
    fold_rows = 2 * FOLDED + per_layer
    sent_rows = FOLDED + per_layer
    samples = slots * devices * ray_depth
    columns = model // HALVES
    slice_rows = rows // groups
    in_vmem = pl.BlockSpec(memory_space=pltpu.VMEM)
    dma = pltpu.SemaphoreType.DMA
    f32, bf16 = jnp.float32, jnp.bfloat16
    vmem = pltpu.VMEM
    colors, loss, head, gain, latent_grad = pl.pallas_call(
        functools.partial(whole_kernel, groups, shards),
        in_specs=[in_vmem] * 10,
        out_specs=[in_vmem] * 5,
        out_shape=[
            jax.ShapeDtypeStruct((3, ray_count), f32),
            jax.ShapeDtypeStruct((1, 1), f32),
            jax.ShapeDtypeStruct((groups, slice_rows, model), bf16),
            jax.ShapeDtypeStruct((shards, rows), f32),
            jax.ShapeDtypeStruct((tokens, model), bf16),
        ],
        scratch_shapes=[
            vmem((devices, 2 * slots + 1, LANES), f32),
            vmem((devices, 2 * slots + 1, LANES), f32),
            vmem((shards, rows, fold_rows), bf16),
            vmem((shards, rows, fold_rows), bf16),
            vmem((model, model), bf16),
            vmem((width // LANES, FOLDED * model // width, LANES), f32),
            vmem((width // LANES, width, LANES), f32),
            vmem((width, 2 * FEATURES), bf16),
            vmem((width, width), bf16),
            vmem((width, width), bf16),
            vmem((width, 4), bf16),
            vmem((8 * FEATURES, LANES), f32),
            vmem((3, samples // LANES, LANES), f32),
            vmem((FEATURES, samples), bf16),
            vmem((width, samples), bf16),
            vmem((width, samples), bf16),
            vmem((4, samples // LANES, LANES), f32),
            vmem((4, samples), f32),
            vmem((FEATURES, width), f32),
            vmem((width, width), f32),
            vmem((devices, 1, LANES), f32),
            vmem((devices, 1, LANES), f32),
            vmem((HALVES, sent_rows, columns), bf16),
            vmem((HALVES, shards, sent_rows, columns), bf16),
            vmem((HALVES, groups, slice_rows, columns), bf16),
            vmem((HALVES, groups, slice_rows, columns), bf16),
            vmem((HALVES, groups, slice_rows, columns), bf16),
            vmem((1, LANES), f32),
            vmem((devices, 1, LANES), f32),
            dma((devices,)),
            dma((devices,)),
            dma((devices,)),
            dma((devices,)),
            dma((devices,)),
            dma((devices,)),
            dma((shards,)),
            dma((shards,)),
            dma((shards,)),
            dma((shards,)),
            dma((shards,)),
            dma((HALVES, shards)),
            dma((HALVES, shards)),
            dma((HALVES, shards)),
            dma((HALVES, groups)),
            dma((HALVES, groups)),
            dma((HALVES, groups)),
            dma((HALVES, groups)),
        ],
        compiler_params=pltpu.CompilerParams(collective_id=1, has_side_effects=True),
    )(
        latents,
        head_weight,
        head_weight.reshape(groups, slice_rows, model),
        norm_gain.reshape(1, model),
        norm_gain.reshape(shards, rows),
        color_head,
        sample_points,
        sample_spacing,
        ray_targets,
        ray_scene.reshape(1, ray_count),
    )
    head_grad = head.astype(f32).reshape(rows, model)
    return (colors, loss[0, 0], head_grad, gain.reshape(model), latent_grad)


def solution(mesh):
    placed = (
        P(("grp", "shard"), None),
        P("shard", None),
        P(),
        P(),
        P(("grp", "shard"), None),
        P(("grp", "shard"), None),
        P(None, ("grp", "shard")),
        P(("grp", "shard")),
    )
    return jax.shard_map(
        body,
        mesh=mesh,
        in_specs=placed,
        out_specs=(
            P(None, ("grp", "shard")),
            P(),
            P("shard", None),
            P(),
            P(("grp", "shard"), None),
        ),
        check_vma=False,
    )
```

time: 125 us -> 85.5 us (0.68)
  local copies, waits for them, and re-layouts: 19.3 us -> 1.89 us
  Pallas kernels: 91.5 us -> 79.1 us
  other arithmetic: 10.2 us -> 1.83 us
    pallas_call x3 -> x1, Pallas kernels: 91.5 us -> 79.1 us  [body(): pl.pallas_call(functools.partial(whole_kernel, groups, shards), in_specs=...]
    reshape x10 -> x0, local copies, waits for them, and re-layouts: 7.54 us -> none  [the longest x1 1.26 us: tail_exchange(): gain = sums[:gain_rows].reshape(model)]
    reduce_sum x4 -> x0, other arithmetic: 4.82 us -> none  [the longest x1 1.61 us: body(): scene_rays = jnp.sum(recv_live)]
    transpose x6 -> x0, local copies, waits for them, and re-layouts: 3.73 us -> none  [the longest x2 1.03 us: render_slots(): target.T[:, :, None]]
    slice x5 -> x0, local copies, waits for them, and re-layouts: 3.36 us -> none  [the longest x1 1.19 us: tail_exchange(): loss = sums[gain_rows, 0]]
    scatter x1 -> x0, other arithmetic: 1.94 us -> none  [body(): jnp.zeros((slot_total, payload.shape[1]), jnp.float32).at[slot_of_ray]]
    reshape x0 -> x1, other arithmetic: none -> 1.83 us  [body(): head_grad = head.astype(f32).reshape(rows, model)]
    unnamed x17 -> x9, local copies, waits for them, and re-layouts: 2.76 us -> 1.89 us
where the time goes in v1:
time: 85.5 us; the launch traced here: 85.3 us
  Pallas kernels  79.1 us (93%)
  between operations  2.48 us (3%)
  local copies, waits for them, and re-layouts  1.89 us (2%)
  other arithmetic  1.83 us (2%)
    pallas_call x1, Pallas kernels, body(): pl.pallas_call(functools.partial(whole_kernel, groups, shards), in_specs=...  79.1 us
    unnamed x9, local copies, waits for them, and re-layouts  1.89 us
    reshape x1, other arithmetic, body(): head_grad = head.astype(f32).reshape(rows, model)  1.83 us

profile of v1, /device:TPU:0, one launch (start us, length us, event | category | flops | bytes accessed | tf_op | source)
XLA Modules:
  0.0 85.3 jit_solution(2770436743412024267)
XLA Ops:
  0.6 79.1 %shard_map.119 = (f32[3,64]{1,0:T(4,128)}, f32[1,1]{1,0:T(1,128)}, bf16[4,32,1024]{2,1,0:T(8,128)(2,1)}, f32[8,128]{1,0:T(8,128)}, bf16[128,1024]{1,0:T(8,128)(2,1)}) custom-call(bf16[128,1024]{1,0:T(8,128)(2,1)} %latent_ref.1, bf16[128,1024]{1,0:T(8,128)(2,1)} %weight_ref.1, bf16[4,32,1024]{2,1,0:T(8,128)(2,1)} %bitcast.9, f32[1,1024]{1,0:T(1,128)} %bitcast.10, ...), custom_call_target="tpu_custom_call" | custom-call | tf_op jit(solution)/shard_map/pallas_call | solution.py:681
  79.7 0.0 copy-start.2
  79.7 0.0 copy-start
  79.8 1.8 %bitcast_convert_fusion = f32[128,1024]{1,0:T(8,128)} fusion(bf16[4,32,1024]{2,1,0:T(8,128)(2,1)} %get-tuple-element.12), kind=kLoop, calls=%fused_computation | loop fusion | flops 131072 | bytes 786432 | tf_op jit(solution)/shard_map/reshape | solution.py:754
  81.6 0.0 copy-done.2
  81.6 0.0 copy-start.1
  81.6 0.6 copy.17
  82.9 0.0 copy-done.1
  82.9 0.6 copy.19
  83.5 0.0 copy-done
  83.5 0.7 copy.20
Async XLA Ops:
  79.7 1.9 %copy-start.2 = (f32[3,64]{1,0:T(4,128)S(1)}, f32[3,64]{1,0:T(4,128)}, u32[]{:S(2)}) copy-start(f32[3,64]{1,0:T(4,128)} %get-tuple-element.20) | copy-start | bytes 2308
  79.7 3.7 %copy-start = (bf16[128,1024]{1,0:T(8,128)(2,1)S(1)}, bf16[128,1024]{1,0:T(8,128)(2,1)}, u32[]{:S(2)}) copy-start(bf16[128,1024]{1,0:T(8,128)(2,1)} %get-tuple-element.24) | copy-start | bytes 786436
  81.6 1.3 %copy-start.1 = (f32[8,128]{1,0:T(8,128)S(1)}, f32[8,128]{1,0:T(8,128)}, u32[]{:S(2)}) copy-start(f32[8,128]{1,0:T(8,128)} %get-tuple-element.13) | copy-start | bytes 12292

commit v2 on v1

--- a/solution.py
+++ b/solution.py
@@ -151,6 +151,12 @@
     return colors, loss * factor
 
 
+def ray_room(devices, shards, ray_count):
+    slots = 4 * ray_count // devices
+    others = pl.cdiv(devices * (ray_count - slots), devices - 1)
+    return pl.cdiv(others, 16) * 16, pl.cdiv(pl.cdiv(slots * devices, shards), 16) * 16
+
+
 def greet_all(groups, shards):
     me = lax.axis_index("grp") * shards + lax.axis_index("shard")
     total = groups * shards
@@ -278,6 +284,14 @@
     grad_ref,
     gain_grad_ref,
     latent_grad_ref,
+    count_row,
+    landed_counts,
+    lead_own,
+    leads,
+    hot_part,
+    hot_parts,
+    hot_piece,
+    hot_all,
     message,
     landed,
     turned_own,
@@ -307,6 +321,16 @@
     done,
     gain_row,
     landed_gain,
+    count_sent,
+    count_arrived,
+    lead_sent,
+    lead_passed,
+    lead_arrived,
+    hot_sent,
+    hot_arrived,
+    piece_sent,
+    piece_passed,
+    piece_arrived,
     message_sent,
     message_arrived,
     shade_sent,
@@ -335,13 +359,13 @@
     width = head_ref.shape[1]
     ray_count, ray_depth = spacing_ref.shape
     slots = 4 * ray_count // total
-    pairs = slots // 2
     fan_scale = width ** (-0.5)
     per_layer = width * width // model
     strips = model // width
     period = FEATURES // strips
     fold_rows = 2 * FOLDED + per_layer
     sent_rows = FOLDED + per_layer
+    own_rays, hot_rays = ray_room(total, shards, ray_count)
     f32 = jnp.float32
     bf16 = jnp.bfloat16
 
@@ -361,10 +385,12 @@
     turned_own[...] = stacked.T.astype(bf16).reshape(turned_own.shape)
 
     scene = scene_ref[...]
+    lane = iota((1, LANES), 1)
     ray_row = iota((ray_count, ray_count), 0)
     ray_column = iota((ray_count, ray_count), 1)
     scene_wide = jnp.broadcast_to(scene, (ray_count, ray_count))
     scene_tall = jnp.sum(jnp.where(ray_row == ray_column, scene_wide, 0), axis=1, keepdims=True)
+    count_row[...] = jnp.sum(jnp.where(scene_tall == lane, 1.0, 0.0), axis=0, keepdims=True)
     same_scene = scene_tall == scene_wide
     rank_wide = jnp.sum(
         jnp.where(jnp.logical_and(same_scene, ray_row < ray_column), 1, 0), axis=0, keepdims=True
@@ -372,47 +398,11 @@
     rank_tall = jnp.sum(
         jnp.where(jnp.logical_and(same_scene, ray_column < ray_row), 1, 0), axis=1, keepdims=True
     )
-    plane_axes = points_ref[:, :LANES]
-    depth_axes = jnp.concatenate([points_ref[:, LANES:], spacing_ref[...]], axis=1)
-    owner = iota((total, ray_count), 0)
-    mine = scene == owner
-    lane = iota((1, LANES), 1)
-    for j in range(slots):
-        chosen = jnp.where(jnp.logical_and(mine, rank_wide == j), 1.0, 0.0)
-        message[:, j, :] = exact(chosen, plane_axes)
-        message[:, slots + j, :] = exact(chosen, depth_axes)
-    spread = jnp.where(iota((3, LANES), 1) // slots == iota((3, LANES), 0), 1.0, 0.0)
-    extra = exact(target_ref[...], spread, (0, 0)) + jnp.where(lane // slots == 3, 1.0, 0.0)
-    extra = jnp.where(rank_tall == lane % slots, extra, 0.0)
-    message[:, 2 * slots, :] = exact(jnp.where(mine, 1.0, 0.0), extra)
     head_t[...] = (head_ref[...].astype(f32) * fan_scale).T.astype(bf16)
     grad_first[...] = jnp.zeros_like(grad_first)
     grad_second[...] = jnp.zeros_like(grad_second)
 
     wait_all()
-
-    def weight_place(origin):
-        return weights.at[pl.ds(pl.multiple_of(origin * rows, rows), rows)]
-
-    def weight_of(origin):
-        return weights[pl.ds(pl.multiple_of(origin * rows, rows), rows), :]
-
-    start_weights, receive_weights, finish_weights = plane_gather(
-        weight_ref, weight_place, weight_sent, weight_passed, weight_arrived
-    )
-    start_messages, receive_messages, finish_messages = messages(
-        groups, shards, lambda other: message.at[other], landed, message_sent, message_arrived
-    )
-    start_weights()
-    start_messages()
-    weights[pl.ds(pl.multiple_of(shard * rows, rows), rows), :] = weight_ref[...]
-    landed[me] = message[me]
-    field_sum = [over_first(turned_own[shard], weight_ref[...])]
-
-    def add_field(origin):
-        field_sum[0] = field_sum[0] + over_first(turned_own[origin], weight_of(origin))
-
-    receive_weights(add_field)
 
     def turned_copy(other, place):
         return pltpu.make_async_remote_copy(
@@ -424,80 +414,194 @@
             device_id_type=MESH,
         )
 
+    def weight_place(origin):
+        return weights.at[pl.ds(pl.multiple_of(origin * rows, rows), rows)]
+
+    def weight_of(origin):
+        return weights[pl.ds(pl.multiple_of(origin * rows, rows), rows), :]
+
     others = [lax.rem(shard + step, shards) for step in range(1, shards)]
+    start_counts, receive_counts, finish_counts = messages(
+        groups, shards, lambda other: count_row, landed_counts, count_sent, count_arrived
+    )
+    start_weights, receive_weights, finish_weights = plane_gather(
+        weight_ref, weight_place, weight_sent, weight_passed, weight_arrived
+    )
+    start_messages, receive_messages, finish_messages = messages(
+        groups, shards, lambda other: message.at[other], landed, message_sent, message_arrived
+    )
+    start_lead, receive_lead, finish_lead = plane_gather(
+        lead_own, lambda origin: leads.at[origin], lead_sent, lead_passed, lead_arrived
+    )
+    start_counts()
     for other in others:
         turned_copy(other, shard).start()
+    start_weights()
+    landed_counts[me] = count_row[...]
     turned[shard] = turned_own[shard]
-
-    field = field_sum[0]
-    first_rows = (field[:FOLDED] + field[FOLDED : 2 * FOLDED]) * fan_scale
-    second_rows = field[2 * FOLDED :].astype(bf16).astype(f32) * fan_scale
-    for m in range(strips):
-        strip = slice(m * width, (m + 1) * width)
-        store_rows(wide_first, m, FOLDED, strips, first_rows[:, strip])
-        store_rows(wide_second, m, per_layer, strips, second_rows[:, strip])
-    first = joined(wide_first)[:FEATURES]
-    wide = joined(wide_second)
-    first_high = first.astype(bf16).astype(f32)
-    first_t[...] = jnp.concatenate([first_high, first - first_high], axis=0).T.astype(bf16)
-    second[...] = wide.astype(bf16)
-    second_t[...] = wide.T.astype(bf16)
+    weights[pl.ds(pl.multiple_of(shard * rows, rows), rows), :] = weight_ref[...]
+
+    receive_counts()
+    counts = landed_counts[:, 0, :]
+    hot_lanes = jnp.min(jnp.where(counts == slots, 1, 0), axis=0, keepdims=True)
+    hot = jnp.sum(jnp.where(hot_lanes > 0, lane, 0), axis=1, keepdims=True)
+    hot_here = hot // shards == group
+    hot_ray = scene == hot
+    hot_target = (hot // shards) * shards + (me * slots + rank_wide) % shards
+    owner = iota((total, ray_count), 0)
+    mine = jnp.where(hot_ray, -1, scene) == owner
+    led = jnp.where(hot_ray, hot_target, -1) == owner
+    payload = jnp.concatenate([points_ref[...], spacing_ref[...]], axis=1)
+    chosen = jnp.concatenate(
+        [jnp.where(jnp.where(mine, rank_wide, -1) == j, 1.0, 0.0) for j in range(slots)]
+        + [jnp.where(led, 1.0, 0.0)],
+        axis=0,
+    )
+    filled = exact(chosen, payload)
+    for j in range(slots + 1):
+        message[:, 2 * j, :] = filled[j * total : (j + 1) * total, :LANES]
+        message[:, 2 * j + 1, :] = filled[j * total : (j + 1) * total, LANES:]
+    spread = jnp.where(iota((3, LANES), 1) % 4 == iota((3, LANES), 0), 1.0, 0.0)
+    extra = exact(target_ref[...], spread, (0, 0)) + jnp.where(lane % 4 == 3, 1.0, 0.0)
+    own_extra = jnp.where(rank_tall == lane // 4, extra, 0.0)
+    hot_extra = jnp.where(lane // 4 == slots, extra, 0.0)
+    message[:, 2 * slots + 2, :] = exact(jnp.where(mine, 1.0, 0.0), own_extra) + exact(
+        jnp.where(led, 1.0, 0.0), hot_extra
+    )
+    start_messages()
+    landed[me] = message[me]
+
+    for other in others:
+        turned_copy(other, other).wait_recv()
+    hot_shard = jnp.where(hot_here, hot % shards, -1)
+    lead = jnp.zeros((rows, fold_rows), f32)
+    for origin in range(shards):
+        lead = lead + jnp.where(hot_shard == origin, turned[origin].astype(f32), 0.0)
+    lead_own[...] = lead.astype(bf16)
+    start_lead()
+    leads[shard] = lead_own[...]
+
+    field_sum = [over_first(turned_own[shard], weight_ref[...])]
+
+    def add_field(origin):
+        field_sum[0] = field_sum[0] + over_first(turned_own[origin], weight_of(origin))
+
+    receive_weights(add_field)
+
+    def set_weights(which, field):
+        first_rows = (field[:FOLDED] + field[FOLDED : 2 * FOLDED]) * fan_scale
+        second_rows = field[2 * FOLDED :].astype(bf16).astype(f32) * fan_scale
+        for m in range(strips):
+            strip = slice(m * width, (m + 1) * width)
+            store_rows(wide_first, m, FOLDED, strips, first_rows[:, strip])
+            store_rows(wide_second, m, per_layer, strips, second_rows[:, strip])
+        first = joined(wide_first)[:FEATURES]
+        wide = joined(wide_second)
+        first_high = first.astype(bf16).astype(f32)
+        first_t[which] = jnp.concatenate([first_high, first - first_high], axis=0).T.astype(bf16)
+        second[which] = wide.astype(bf16)
+        second_t[which] = wide.T.astype(bf16)
+
+    set_weights(0, field_sum[0])
 
     receive_messages()
-    flat = jnp.concatenate([landed[:, j, :] for j in range(slots)], axis=0)
-    deep = jnp.concatenate([landed[:, slots + j, :] for j in range(slots)], axis=0)
-    extras = landed[:, 2 * slots, :]
-    half_rows = pairs * total
+    wanted = jnp.where(lane == me, 1.0, 0.0) * jnp.where(hot == me, 0.0, 1.0)
+    numbers = exact(jnp.broadcast_to(wanted, (8, LANES)), counts, (1, 1))
+    before = jnp.where(iota((total, total), 0) < iota((total, total), 1), 1.0, 0.0)
+    offsets = exact(numbers, before)[0:1]
+    numbers = numbers[0:1]
+    extras = landed[:, 2 * slots + 2, :]
+
+    def arrived_slot(j):
+        lifted = extras if j == 0 else pltpu.roll(extras, LANES - 4 * j, 1)
+        return jnp.concatenate([landed[:, 2 * j, :], landed[:, 2 * j + 1, :], lifted], axis=1)
+
+    slot_row = iota((own_rays, total), 0).astype(f32)
+    keeps = [
+        jnp.where(jnp.where(numbers > j, offsets + j, -1.0) == slot_row, 1.0, 0.0)
+        for j in range(slots)
+    ]
+    own_slots = sum(exact(keeps[j], arrived_slot(j)) for j in range(slots))
+    hot_place = (iota((hot_rays, total), 0) * shards + shard) // slots
+    hot_keep = jnp.where(hot_place == iota((hot_rays, total), 1), 1.0, 0.0)
+    hot_slots = exact(hot_keep, arrived_slot(slots))
+    own_pairs, hot_pairs = own_rays // 2, hot_rays // 2
+    all_pairs = own_pairs + hot_pairs
+    lower = jnp.concatenate([own_slots[:own_pairs], hot_slots[:hot_pairs]], axis=0)
+    upper = jnp.concatenate([own_slots[own_pairs:], hot_slots[hot_pairs:]], axis=0)
     low = lane < ray_depth
 
-    def unpack(values):
-        lower, upper = values[:half_rows], values[half_rows:]
+    def unpack(at):
+        left, right = lower[:, at : at + LANES], upper[:, at : at + LANES]
         return (
-            jnp.where(low, lower, pltpu.roll(upper, ray_depth, 1)),
-            jnp.where(low, pltpu.roll(lower, ray_depth, 1), upper),
-        )
-
-    coords[0], coords[1] = unpack(flat)
-    coords[2], spacing = unpack(deep)
+            jnp.where(low, left, pltpu.roll(right, ray_depth, 1)),
+            jnp.where(low, pltpu.roll(left, ray_depth, 1), right),
+        )
+
+    coords[0], coords[1] = unpack(0)
+    coords[2], spacing = unpack(LANES)
 
     def widen(c):
-        return jnp.concatenate(
-            [
-                jnp.where(
-                    low,
-                    extras[:, c * slots + j : c * slots + j + 1],
-                    extras[:, c * slots + j + pairs : c * slots + j + pairs + 1],
-                )
-                for j in range(pairs)
-            ],
-            axis=0,
-        )
-
-    scene_rays = jnp.sum(
-        jnp.where(lane // slots == 3, extras, 0.0), axis=(0, 1), keepdims=True
-    )
-    factor = widen(3) / (total * scene_rays)
+        at = 2 * LANES + c
+        return jnp.where(low, lower[:, at : at + 1], upper[:, at : at + 1])
+
+    own_count = jnp.sum(numbers, axis=1, keepdims=True)
+    own_factor = 1.0 / (total * jnp.maximum(own_count, 1.0))
+    hot_factor = 1.0 / (total * total * slots)
+    factor = widen(3) * jnp.where(iota((all_pairs, 1), 0) < own_pairs, own_factor, hot_factor)
     targets = [widen(c) for c in range(3)]
-    blocks = half_rows * LANES // BLOCK
-
-    def forward(i, carry):
-        forward_block(
-            i, coords, first_t, second_t, head_ref, encoded, zeros_all, ones_all, twos_all, raw
-        )
-        return carry
-
-    lax.fori_loop(0, blocks, forward, 0)
+    own_blocks = own_pairs // 8
+    blocks = all_pairs // 8
+
+    def forward(which):
+        def step(i, carry):
+            forward_block(
+                i,
+                coords,
+                first_t.at[which],
+                second_t.at[which],
+                head_ref,
+                encoded,
+                zeros_all,
+                ones_all,
+                twos_all,
+                raw,
+            )
+            return carry
+
+        return step
+
+    lax.fori_loop(0, own_blocks, forward(0), 0)
+    lead_field = [over_first(lead_own[...], weight_ref[...])]
+
+    def add_lead(origin):
+        lead_field[0] = lead_field[0] + over_first(leads[origin], weight_of(origin))
+
+    receive_lead(add_lead)
+    set_weights(1, lead_field[0])
+    lax.fori_loop(own_blocks, blocks, forward(1), 0)
     colors, losses = render_middle(ray_depth, raw, spacing, targets, factor, draw)
     shade = jnp.where(
-        lane == 3 * slots, jnp.sum(losses, axis=(0, 1), keepdims=True) * (1.0 / ray_depth), 0.0
-    )
-    shade = jnp.broadcast_to(shade, (total, LANES))
-    for c in range(3):
-        for j in range(pairs):
-            values = colors[c][j * total : (j + 1) * total]
-            at = c * slots + j
-            shade = jnp.where(lane == at, values[:, 0:1], shade)
-            shade = jnp.where(lane == at + pairs, values[:, ray_depth : ray_depth + 1], shade)
+        lane == 4 * slots + 4,
+        jnp.sum(losses, axis=(0, 1), keepdims=True) * (1.0 / ray_depth),
+        0.0,
+    )
+
+    def color_rows(start, stop):
+        columns = []
+        for side in (0, ray_depth):
+            values = jnp.zeros((stop - start, LANES), f32)
+            for c in range(3):
+                values = jnp.where(lane == c, colors[c][start:stop, side : side + 1], values)
+            columns.append(values)
+        return jnp.concatenate(columns, axis=0)
+
+    own_colors = color_rows(0, own_pairs)
+    hot_colors = color_rows(own_pairs, all_pairs)
+    for j in range(slots):
+        back = exact(keeps[j], own_colors, (0, 0))
+        shade = shade + (back if j == 0 else pltpu.roll(back, 4 * j, 1))
+    shade = shade + pltpu.roll(exact(hot_keep, hot_colors, (0, 0)), 4 * slots, 1)
     shades[:, 0, :] = shade
     start_shades, receive_shades, finish_shades = messages(
         groups, shards, lambda other: shades.at[other], landed_shades, shade_sent, shade_arrived
@@ -505,25 +609,54 @@
     start_shades()
     landed_shades[me] = shades[me]
 
-    def backward(i, carry):
-        backward_block(
-            i, draw, second, head_t, zeros_all, ones_all, twos_all, grad_first, grad_second
-        )
-        return carry
-
-    lax.fori_loop(0, blocks, backward, 0)
-
-    for lanes in range(width // LANES):
-        wide_first[lanes, :FEATURES, :] = grad_first[:, lanes * LANES : (lanes + 1) * LANES]
-        wide_second[lanes] = grad_second[:, lanes * LANES : (lanes + 1) * LANES]
+    def backward(which):
+        def step(i, carry):
+            backward_block(
+                i, draw, second.at[which], head_t, zeros_all, ones_all, twos_all, grad_first, grad_second
+            )
+            return carry
+
+        return step
+
     columns = model // HALVES
-    for m in range(strips):
+    piece = model // shards
+
+    def field_strips():
+        for lanes in range(width // LANES):
+            at = slice(lanes * LANES, (lanes + 1) * LANES)
+            wide_first[lanes, :FEATURES, :] = grad_first[:, at]
+            wide_second[lanes] = grad_second[:, at]
+        strip_values = []
+        for m in range(strips):
+            head_rows = load_rows(wide_first, m, FOLDED, strips)
+            head_rows = jnp.where(iota((FOLDED, 1), 0) < period, head_rows, 0.0)
+            strip_values.append(
+                jnp.concatenate([head_rows, load_rows(wide_second, m, per_layer, strips)], axis=0)
+            )
+        return strip_values
+
+    def hot_copy(other, place):
+        return pltpu.make_async_remote_copy(
+            src_ref=hot_part.at[other],
+            dst_ref=hot_parts.at[place],
+            send_sem=hot_sent.at[other],
+            recv_sem=hot_arrived.at[place],
+            device_id=(group, other),
+            device_id_type=MESH,
+        )
+
+    lax.fori_loop(own_blocks, blocks, backward(1), 0)
+    hot_strips = jnp.concatenate(field_strips(), axis=1)
+    for p in range(shards):
+        hot_part[p] = hot_strips[:, p * piece : (p + 1) * piece].astype(bf16)
+    for other in others:
+        hot_copy(other, shard).start()
+    grad_first[...] = jnp.zeros_like(grad_first)
+    grad_second[...] = jnp.zeros_like(grad_second)
+    lax.fori_loop(0, own_blocks, backward(0), 0)
+    for m, values in enumerate(field_strips()):
         half, place = divmod(m * width, columns)
-        strip = slice(place, place + width)
-        head_rows = load_rows(wide_first, m, FOLDED, strips)
-        head_rows = jnp.where(iota((FOLDED, 1), 0) < period, head_rows, 0.0)
-        d_field[half, :FOLDED, strip] = head_rows.astype(bf16)
-        d_field[half, FOLDED:, strip] = load_rows(wide_second, m, per_layer, strips).astype(bf16)
+        d_field[half, :, place : place + width] = values.astype(bf16)
 
     gathers = [
         plane_gather(
@@ -537,9 +670,16 @@
     ]
     for half in range(HALVES):
         gathers[half][0]()
-
+    piece_sum = hot_part[shard].astype(f32)
     for other in others:
-        turned_copy(other, other).wait_recv()
+        hot_copy(other, other).wait_recv()
+        piece_sum = piece_sum + hot_parts[other].astype(f32)
+    hot_piece[...] = piece_sum.astype(bf16)
+    start_hot, receive_hot, finish_hot = plane_gather(
+        hot_piece, lambda origin: hot_all.at[origin], piece_sent, piece_passed, piece_arrived
+    )
+    start_hot()
+    hot_all[shard] = hot_piece[...]
 
     group_steps = [lax.rem(group + step, groups) for step in range(1, groups)]
 
@@ -574,6 +714,16 @@
             head_sum[0] = head_sum[0] + head_term(origin, fields[half, origin])
 
         gathers[half][1](add_head)
+        if half == 0:
+            receive_hot(lambda origin: None)
+        per_half = shards // HALVES
+        hot_values = jnp.concatenate(
+            [hot_all[p] for p in range(half * per_half, (half + 1) * per_half)], axis=1
+        )
+        hot_top = hot_values[:FOLDED]
+        head_sum[0] = head_sum[0] + product(
+            lead_own[...], jnp.concatenate([hot_top, hot_top, hot_values[FOLDED:]], axis=0)
+        )
         part[half] = head_sum[0].astype(bf16).reshape(part.shape[1:])
         for other in group_steps:
             part_copy(half, other, group).start()
@@ -607,6 +757,8 @@
     source = jnp.where(token < per_layer, token % period, token - per_layer + FOLDED)
     copies = jnp.where(source == iota((tokens, sent_rows), 1), 1.0, 0.0).astype(bf16)
     own_field = jnp.concatenate([d_field[half] for half in range(HALVES)], axis=1)
+    hot_field = jnp.concatenate([hot_all[p] for p in range(shards)], axis=1)
+    own_field = jnp.where(hot == me, hot_field.astype(f32), own_field.astype(f32)).astype(bf16)
     d_norm = over_last(product(copies, own_field).astype(bf16), weights[...])
     latent = latent_ref[...].astype(f32)
     inv_rms = lax.rsqrt(jnp.mean(latent * latent, axis=1, keepdims=True) + norm_eps)
@@ -619,13 +771,16 @@
     receive_shades()
     returned = landed_shades[:, 0, :]
     loss_ref[...] = jnp.sum(
-        jnp.where(lane == 3 * slots, returned, 0.0), axis=(0, 1), keepdims=True
-    )
-    picked = exact(returned, jnp.where(mine, 1.0, 0.0), (0, 0))
+        jnp.where(lane == 4 * slots + 4, returned, 0.0), axis=(0, 1), keepdims=True
+    )
+    picked = exact(
+        returned, jnp.where(mine, 1.0, 0.0) + jnp.where(led, 1.0, 0.0), (0, 0)
+    )
+    first_place = jnp.where(hot_ray, 4 * slots, 4 * rank_wide)
     place = iota((LANES, ray_count), 0)
     for c in range(3):
         color_ref[c : c + 1, :] = jnp.sum(
-            jnp.where(place == c * slots + rank_wide, picked, 0.0), axis=0, keepdims=True
+            jnp.where(place == first_place + c, picked, 0.0), axis=0, keepdims=True
         )
 
     for half in range(HALVES):
@@ -638,8 +793,13 @@
     gains = jnp.concatenate([gains[g * shards : (g + 1) * shards] for g in range(groups)], axis=1)
     gain_grad_ref[...] = gains / gain_rows_ref[...]
 
+    finish_counts()
     finish_weights()
     finish_messages()
+    finish_lead()
+    finish_hot()
+    for other in others:
+        hot_copy(other, shard).wait_send()
     finish_shades()
     finish_gain()
     for other in others:
@@ -671,7 +831,7 @@
     per_layer = width * width // model
     fold_rows = 2 * FOLDED + per_layer
     sent_rows = FOLDED + per_layer
-    samples = slots * devices * ray_depth
+    samples = sum(ray_room(devices, shards, ray_count)) * ray_depth
     columns = model // HALVES
     slice_rows = rows // groups
     in_vmem = pl.BlockSpec(memory_space=pltpu.VMEM)
@@ -690,16 +850,24 @@
             jax.ShapeDtypeStruct((tokens, model), bf16),
         ],
         scratch_shapes=[
-            vmem((devices, 2 * slots + 1, LANES), f32),
-            vmem((devices, 2 * slots + 1, LANES), f32),
+            vmem((1, LANES), f32),
+            vmem((devices, 1, LANES), f32),
+            vmem((rows, fold_rows), bf16),
+            vmem((shards, rows, fold_rows), bf16),
+            vmem((shards, sent_rows, rows), bf16),
+            vmem((shards, sent_rows, rows), bf16),
+            vmem((sent_rows, rows), bf16),
+            vmem((shards, sent_rows, rows), bf16),
+            vmem((devices, 2 * slots + 3, LANES), f32),
+            vmem((devices, 2 * slots + 3, LANES), f32),
             vmem((shards, rows, fold_rows), bf16),
             vmem((shards, rows, fold_rows), bf16),
             vmem((model, model), bf16),
             vmem((width // LANES, FOLDED * model // width, LANES), f32),
             vmem((width // LANES, width, LANES), f32),
-            vmem((width, 2 * FEATURES), bf16),
-            vmem((width, width), bf16),
-            vmem((width, width), bf16),
+            vmem((2, width, 2 * FEATURES), bf16),
+            vmem((2, width, width), bf16),
+            vmem((2, width, width), bf16),
             vmem((width, 4), bf16),
             vmem((8 * FEATURES, LANES), f32),
             vmem((3, samples // LANES, LANES), f32),
@@ -721,6 +889,16 @@
             vmem((devices, 1, LANES), f32),
             dma((devices,)),
             dma((devices,)),
+            dma((shards,)),
+            dma((shards,)),
+            dma((shards,)),
+            dma((shards,)),
+            dma((shards,)),
+            dma((shards,)),
+            dma((shards,)),
+            dma((shards,)),
+            dma((devices,)),
+            dma((devices,)),
             dma((devices,)),
             dma((devices,)),
             dma((devices,)),

time: 85.5 us -> 81.2 us (0.950)
  Pallas kernels: 79.1 us -> 74.8 us
    pallas_call x1, Pallas kernels: 79.1 us -> 74.8 us  [body(): pl.pallas_call(functools.partial(whole_kernel, groups, shards), in_specs=...]
where the time goes in v2:
time: 81.2 us; the launch traced here: 81 us
  Pallas kernels  74.8 us (92%)
  between operations  2.48 us (3%)
  local copies, waits for them, and re-layouts  1.89 us (2%)
  other arithmetic  1.83 us (2%)
    pallas_call x1, Pallas kernels, body(): pl.pallas_call(functools.partial(whole_kernel, groups, shards), in_specs=...  74.8 us
    unnamed x9, local copies, waits for them, and re-layouts  1.89 us
    reshape x1, other arithmetic, body(): head_grad = head.astype(f32).reshape(rows, model)  1.83 us

profile of v2, /device:TPU:0, one launch (start us, length us, event | category | flops | bytes accessed | tf_op | source)
XLA Modules:
  0.0 81.0 jit_solution(7486651629308524690)
XLA Ops:
  0.6 74.8 %shard_map.119 = (f32[3,64]{1,0:T(4,128)}, f32[1,1]{1,0:T(1,128)}, bf16[4,32,1024]{2,1,0:T(8,128)(2,1)}, f32[8,128]{1,0:T(8,128)}, bf16[128,1024]{1,0:T(8,128)(2,1)}) custom-call(bf16[128,1024]{1,0:T(8,128)(2,1)} %latent_ref.1, bf16[128,1024]{1,0:T(8,128)(2,1)} %weight_ref.1, bf16[4,32,1024]{2,1,0:T(8,128)(2,1)} %bitcast.9, f32[1,1024]{1,0:T(1,128)} %bitcast.10, ...), custom_call_target="tpu_custom_call" | custom-call | tf_op jit(solution)/shard_map/pallas_call | solution.py:841
  75.5 0.0 copy-start.2
  75.5 0.0 copy-start
  75.5 1.8 %bitcast_convert_fusion = f32[128,1024]{1,0:T(8,128)} fusion(bf16[4,32,1024]{2,1,0:T(8,128)(2,1)} %get-tuple-element.12), kind=kLoop, calls=%fused_computation | loop fusion | flops 131072 | bytes 786432 | tf_op jit(solution)/shard_map/reshape | solution.py:932
  77.3 0.0 copy-done.2
  77.3 0.0 copy-start.1
  77.3 0.6 copy.17
  78.6 0.0 copy-done.1
  78.6 0.6 copy.19
  79.2 0.0 copy-done
  79.2 0.7 copy.20
Async XLA Ops:
  75.5 1.9 %copy-start.2 = (f32[3,64]{1,0:T(4,128)S(1)}, f32[3,64]{1,0:T(4,128)}, u32[]{:S(2)}) copy-start(f32[3,64]{1,0:T(4,128)} %get-tuple-element.20) | copy-start | bytes 2308
  75.5 3.7 %copy-start = (bf16[128,1024]{1,0:T(8,128)(2,1)S(1)}, bf16[128,1024]{1,0:T(8,128)(2,1)}, u32[]{:S(2)}) copy-start(bf16[128,1024]{1,0:T(8,128)(2,1)} %get-tuple-element.24) | copy-start | bytes 786436
  77.3 1.3 %copy-start.1 = (f32[8,128]{1,0:T(8,128)S(1)}, f32[8,128]{1,0:T(8,128)}, u32[]{:S(2)}) copy-start(f32[8,128]{1,0:T(8,128)} %get-tuple-element.13) | copy-start | bytes 12292

commit v3 on v2

--- a/solution.py
+++ b/solution.py
@@ -41,6 +41,33 @@
         preferred_element_type=jnp.float32,
         precision=lax.Precision.HIGHEST,
     )
+
+
+def select(onehot, values, contract=(1, 0)):
+    total = 0.0
+    for _ in range(3):
+        term = values.astype(jnp.bfloat16)
+        values = values - term.astype(jnp.float32)
+        total = total + lax.dot_general(
+            onehot,
+            term,
+            (((contract[0],), (contract[1],)), ((), ())),
+            preferred_element_type=jnp.float32,
+        )
+    return total
+
+
+def over_first_select(values, onehot):
+    total = 0.0
+    for _ in range(3):
+        term = values.astype(jnp.bfloat16)
+        values = values - term.astype(jnp.float32)
+        total = total + over_first(term, onehot)
+    return total
+
+
+def chosen_as(mask):
+    return jnp.where(mask, 1.0, 0.0).astype(jnp.bfloat16)
 
 
 def over_first(a, b):
@@ -177,37 +204,28 @@
     me = lax.axis_index("grp") * shards + lax.axis_index("shard")
     total = groups * shards
 
-    def copy(other, place):
-        return pltpu.make_async_remote_copy(
-            src_ref=source(other),
-            dst_ref=landed.at[place],
-            send_sem=sent.at[other],
-            recv_sem=arrived.at[place],
-            device_id=(other // shards, lax.rem(other, shards)),
-            device_id_type=MESH,
-        )
-
     def start():
         def one(step, carry):
-            copy(lax.rem(me + step, total), me).start()
+            other = lax.rem(me + step, total)
+            pltpu.make_async_remote_copy(
+                src_ref=source(other),
+                dst_ref=landed.at[me],
+                send_sem=sent,
+                recv_sem=arrived,
+                device_id=(other // shards, lax.rem(other, shards)),
+                device_id_type=MESH,
+            ).start()
             return carry
 
         lax.fori_loop(1, total, one, 0)
 
+    everything = landed.at[pl.ds(0, total - 1)]
+
     def receive():
-        def one(step, carry):
-            other = lax.rem(me + total - step, total)
-            copy(other, other).wait_recv()
-            return carry
-
-        lax.fori_loop(1, total, one, 0)
+        pltpu.make_async_copy(everything, everything, arrived).wait()
 
     def finish():
-        def one(step, carry):
-            copy(lax.rem(me + step, total), me).wait_send()
-            return carry
-
-        lax.fori_loop(1, total, one, 0)
+        pltpu.make_async_copy(everything, everything, sent).wait()
 
     return start, receive, finish
 
@@ -457,16 +475,16 @@
         + [jnp.where(led, 1.0, 0.0)],
         axis=0,
     )
-    filled = exact(chosen, payload)
+    filled = select(chosen.astype(bf16), payload)
     for j in range(slots + 1):
         message[:, 2 * j, :] = filled[j * total : (j + 1) * total, :LANES]
         message[:, 2 * j + 1, :] = filled[j * total : (j + 1) * total, LANES:]
     spread = jnp.where(iota((3, LANES), 1) % 4 == iota((3, LANES), 0), 1.0, 0.0)
-    extra = exact(target_ref[...], spread, (0, 0)) + jnp.where(lane % 4 == 3, 1.0, 0.0)
+    extra = over_first_select(target_ref[...], spread.astype(bf16)) + jnp.where(lane % 4 == 3, 1.0, 0.0)
     own_extra = jnp.where(rank_tall == lane // 4, extra, 0.0)
     hot_extra = jnp.where(lane // 4 == slots, extra, 0.0)
-    message[:, 2 * slots + 2, :] = exact(jnp.where(mine, 1.0, 0.0), own_extra) + exact(
-        jnp.where(led, 1.0, 0.0), hot_extra
+    message[:, 2 * slots + 2, :] = select(chosen_as(mine), own_extra) + select(
+        chosen_as(led), hot_extra
     )
     start_messages()
     landed[me] = message[me]
@@ -506,25 +524,25 @@
 
     receive_messages()
     wanted = jnp.where(lane == me, 1.0, 0.0) * jnp.where(hot == me, 0.0, 1.0)
-    numbers = exact(jnp.broadcast_to(wanted, (8, LANES)), counts, (1, 1))
-    before = jnp.where(iota((total, total), 0) < iota((total, total), 1), 1.0, 0.0)
-    offsets = exact(numbers, before)[0:1]
-    numbers = numbers[0:1]
+    many = slots * total
+    tall_counts = jnp.concatenate([counts] * slots, axis=0).astype(bf16)
+    wanted = jnp.broadcast_to(wanted, (8, LANES)).astype(bf16)
+    wide_numbers = over_last(wanted, tall_counts)[0:1]
+    earlier = chosen_as(iota((total, many), 0) < iota((total, many), 1) % total)
+    offsets = product(over_last(wanted, counts.astype(bf16)).astype(bf16), earlier)[0:1]
     extras = landed[:, 2 * slots + 2, :]
 
     def arrived_slot(j):
         lifted = extras if j == 0 else pltpu.roll(extras, LANES - 4 * j, 1)
         return jnp.concatenate([landed[:, 2 * j, :], landed[:, 2 * j + 1, :], lifted], axis=1)
 
-    slot_row = iota((own_rays, total), 0).astype(f32)
-    keeps = [
-        jnp.where(jnp.where(numbers > j, offsets + j, -1.0) == slot_row, 1.0, 0.0)
-        for j in range(slots)
-    ]
-    own_slots = sum(exact(keeps[j], arrived_slot(j)) for j in range(slots))
+    slot_of = (iota((1, many), 1) // total).astype(f32)
+    slot_at = jnp.where(wide_numbers > slot_of, offsets + slot_of, -1.0)
+    keep = chosen_as(slot_at == iota((own_rays, many), 0).astype(f32))
+    own_slots = select(keep, jnp.concatenate([arrived_slot(j) for j in range(slots)], axis=0))
     hot_place = (iota((hot_rays, total), 0) * shards + shard) // slots
-    hot_keep = jnp.where(hot_place == iota((hot_rays, total), 1), 1.0, 0.0)
-    hot_slots = exact(hot_keep, arrived_slot(slots))
+    hot_keep = chosen_as(hot_place == iota((hot_rays, total), 1))
+    hot_slots = select(hot_keep, arrived_slot(slots))
     own_pairs, hot_pairs = own_rays // 2, hot_rays // 2
     all_pairs = own_pairs + hot_pairs
     lower = jnp.concatenate([own_slots[:own_pairs], hot_slots[:hot_pairs]], axis=0)
@@ -545,7 +563,7 @@
         at = 2 * LANES + c
         return jnp.where(low, lower[:, at : at + 1], upper[:, at : at + 1])
 
-    own_count = jnp.sum(numbers, axis=1, keepdims=True)
+    own_count = jnp.sum(jnp.where(slot_of == 0.0, wide_numbers, 0.0), axis=1, keepdims=True)
     own_factor = 1.0 / (total * jnp.maximum(own_count, 1.0))
     hot_factor = 1.0 / (total * total * slots)
     factor = widen(3) * jnp.where(iota((all_pairs, 1), 0) < own_pairs, own_factor, hot_factor)
@@ -598,10 +616,11 @@
 
     own_colors = color_rows(0, own_pairs)
     hot_colors = color_rows(own_pairs, all_pairs)
+    back = select(keep, own_colors, (0, 0))
     for j in range(slots):
-        back = exact(keeps[j], own_colors, (0, 0))
-        shade = shade + (back if j == 0 else pltpu.roll(back, 4 * j, 1))
-    shade = shade + pltpu.roll(exact(hot_keep, hot_colors, (0, 0)), 4 * slots, 1)
+        part_back = back[j * total : (j + 1) * total]
+        shade = shade + (part_back if j == 0 else pltpu.roll(part_back, 4 * j, 1))
+    shade = shade + pltpu.roll(select(hot_keep, hot_colors, (0, 0)), 4 * slots, 1)
     shades[:, 0, :] = shade
     start_shades, receive_shades, finish_shades = messages(
         groups, shards, lambda other: shades.at[other], landed_shades, shade_sent, shade_arrived
@@ -668,8 +687,7 @@
         )
         for half in range(HALVES)
     ]
-    for half in range(HALVES):
-        gathers[half][0]()
+    gathers[0][0]()
     piece_sum = hot_part[shard].astype(f32)
     for other in others:
         hot_copy(other, other).wait_recv()
@@ -679,6 +697,8 @@
         hot_piece, lambda origin: hot_all.at[origin], piece_sent, piece_passed, piece_arrived
     )
     start_hot()
+    for half in range(1, HALVES):
+        gathers[half][0]()
     hot_all[shard] = hot_piece[...]
 
     group_steps = [lax.rem(group + step, groups) for step in range(1, groups)]
@@ -735,22 +755,26 @@
         for other in group_steps:
             part_copy(half, other, other).wait_recv()
             slice_sum = slice_sum + parts[half, other].astype(f32)
+        weight = weight_part_ref[group][:, half * columns : (half + 1) * columns].astype(f32)
+        gain_terms.append(jnp.sum(slice_sum * weight, axis=1, keepdims=True))
+        if half == HALVES - 1:
+            same_row = iota((slice_rows, slice_rows), 0) == iota((slice_rows, slice_rows), 1)
+            gain_row[0:1, :slice_rows] = jnp.sum(
+                jnp.where(same_row, sum(gain_terms), 0.0), axis=0, keepdims=True
+            )
+            start_gain()
         done[half, group] = slice_sum.astype(bf16)
         for other in group_steps:
             done_copy(half, other, group).start()
-        weight = weight_part_ref[group][:, half * columns : (half + 1) * columns].astype(f32)
-        gain_terms.append(exact(jnp.ones((8, columns), f32), slice_sum * weight, (1, 1)))
-
+
+    slice_rows = rows // groups
+    start_gain, receive_gain, finish_gain = messages(
+        groups, shards, lambda other: gain_row, landed_gain, gain_sent, gain_arrived
+    )
     gather_half(0)
     gather_half(1)
     sum_half(0)
     sum_half(1)
-    slice_rows = rows // groups
-    gain_row[0:1, :slice_rows] = (gain_terms[0] + gain_terms[1])[0:1]
-    start_gain, receive_gain, finish_gain = messages(
-        groups, shards, lambda other: gain_row, landed_gain, gain_sent, gain_arrived
-    )
-    start_gain()
     landed_gain[me] = gain_row[...]
 
     token = iota((tokens, sent_rows), 0)
@@ -773,9 +797,7 @@
     loss_ref[...] = jnp.sum(
         jnp.where(lane == 4 * slots + 4, returned, 0.0), axis=(0, 1), keepdims=True
     )
-    picked = exact(
-        returned, jnp.where(mine, 1.0, 0.0) + jnp.where(led, 1.0, 0.0), (0, 0)
-    )
+    picked = over_first_select(returned, chosen_as(mine) + chosen_as(led))
     first_place = jnp.where(hot_ray, 4 * slots, 4 * rank_wide)
     place = iota((LANES, ray_count), 0)
     for c in range(3):
@@ -887,22 +909,22 @@
             vmem((HALVES, groups, slice_rows, columns), bf16),
             vmem((1, LANES), f32),
             vmem((devices, 1, LANES), f32),
-            dma((devices,)),
-            dma((devices,)),
-            dma((shards,)),
-            dma((shards,)),
-            dma((shards,)),
-            dma((shards,)),
-            dma((shards,)),
-            dma((shards,)),
-            dma((shards,)),
-            dma((shards,)),
-            dma((devices,)),
-            dma((devices,)),
-            dma((devices,)),
-            dma((devices,)),
-            dma((devices,)),
-            dma((devices,)),
+            dma,
+            dma,
+            dma((shards,)),
+            dma((shards,)),
+            dma((shards,)),
+            dma((shards,)),
+            dma((shards,)),
+            dma((shards,)),
+            dma((shards,)),
+            dma((shards,)),
+            dma,
+            dma,
+            dma,
+            dma,
+            dma,
+            dma,
             dma((shards,)),
             dma((shards,)),
             dma((shards,)),
@@ -929,8 +951,40 @@
         ray_targets,
         ray_scene.reshape(1, ray_count),
     )
-    head_grad = head.astype(f32).reshape(rows, model)
+    colors, loss, head_grad, gain, latent_grad = hand_out(colors, loss, head, gain, latent_grad)
     return (colors, loss[0, 0], head_grad, gain.reshape(model), latent_grad)
+
+
+def hand_out_kernel(color_in, loss_in, head_in, gain_in, latent_in, color, loss, head, gain, latent):
+    color[...] = color_in[...]
+    loss[...] = loss_in[...]
+    gain[...] = gain_in[...]
+    head[...] = head_in[0].astype(jnp.float32)
+    latent[...] = latent_in[...]
+
+
+def hand_out(colors, loss, head, gain, latent_grad):
+    groups, slice_rows, model = head.shape
+    tokens = latent_grad.shape[0]
+    fixed = lambda i: (0, 0)
+    by_row = lambda i: (i, 0)
+    small = [pl.BlockSpec(colors.shape, fixed), pl.BlockSpec(loss.shape, fixed)]
+    gain_spec = pl.BlockSpec(gain.shape, fixed)
+    latent_spec = pl.BlockSpec((tokens // groups, model), by_row)
+    return pl.pallas_call(
+        hand_out_kernel,
+        grid=(groups,),
+        in_specs=small
+        + [pl.BlockSpec((1, slice_rows, model), lambda i: (i, 0, 0)), gain_spec, latent_spec],
+        out_specs=small + [pl.BlockSpec((slice_rows, model), by_row), gain_spec, latent_spec],
+        out_shape=[
+            jax.ShapeDtypeStruct(colors.shape, colors.dtype),
+            jax.ShapeDtypeStruct(loss.shape, loss.dtype),
+            jax.ShapeDtypeStruct((groups * slice_rows, model), jnp.float32),
+            jax.ShapeDtypeStruct(gain.shape, gain.dtype),
+            jax.ShapeDtypeStruct(latent_grad.shape, latent_grad.dtype),
+        ],
+    )(colors, loss, head, gain, latent_grad)
 
 
 def solution(mesh):

time: 81.2 us -> 71.5 us (0.88)
  Pallas kernels: 74.8 us -> 70.5 us
  local copies, waits for them, and re-layouts: 1.89 us -> 0 us
  between operations: 2.48 us -> 0.64 us
  other arithmetic: 1.83 us -> 0 us
    pallas_call x1, Pallas kernels: 74.8 us -> 66.8 us  [body(): pl.pallas_call(functools.partial(whole_kernel, groups, shards), in_specs=...]
    pallas_call x0 -> x1, Pallas kernels: none -> 3.71 us  [hand_out(): pl.pallas_call(hand_out_kernel, grid=(groups,), in_specs=small + [pl.Bloc...]
    unnamed x9 -> x0, local copies, waits for them, and re-layouts: 1.89 us -> none
    reshape x1 -> x0, other arithmetic: 1.83 us -> none  [body(): head_grad = head.astype(f32).reshape(rows, model)]
where the time goes in v3:
time: 71.5 us; the launch traced here: 71.2 us
  Pallas kernels  70.5 us (99%)
    pallas_call x1, Pallas kernels, body(): pl.pallas_call(functools.partial(whole_kernel, groups, shards), in_specs=...  66.8 us
    pallas_call x1, Pallas kernels, hand_out(): pl.pallas_call(hand_out_kernel, grid=(groups,), in_specs=small + [pl.Bloc...  3.71 us

profile of v3, /device:TPU:0, one launch (start us, length us, event | category | flops | bytes accessed | tf_op | source)
XLA Modules:
  0.0 71.2 jit_solution(16993191335720451669)
XLA Ops:
  0.6 66.8 %shard_map.119 = (f32[3,64]{1,0:T(4,128)}, f32[1,1]{1,0:T(1,128)}, bf16[4,32,1024]{2,1,0:T(8,128)(2,1)}, f32[8,128]{1,0:T(8,128)}, bf16[128,1024]{1,0:T(8,128)(2,1)}) custom-call(bf16[128,1024]{1,0:T(8,128)(2,1)} %latent_ref.1, bf16[128,1024]{1,0:T(8,128)(2,1)} %weight_ref.1, bf16[4,32,1024]{2,1,0:T(8,128)(2,1)} %bitcast.6, f32[1,1024]{1,0:T(1,128)} %bitcast.7, ...), custom_call_target="tpu_custom_call" | custom-call | tf_op jit(solution)/shard_map/pallas_call | solution.py:863
  67.5 3.7 %shard_map.120 = (f32[3,64]{1,0:T(4,128)}, f32[1,1]{1,0:T(1,128)}, f32[128,1024]{1,0:T(8,128)}, f32[8,128]{1,0:T(8,128)}, bf16[128,1024]{1,0:T(8,128)(2,1)}) custom-call(f32[3,64]{1,0:T(4,128)} %get-tuple-element.15.color_in, f32[1,1]{1,0:T(1,128)} %get-tuple-element.16.loss_in, bf16[4,32,1024]{2,1,0:T(8,128)(2,1)} %get-tuple-element.17.head_in, ...), custom_call_target="tpu_custom_call" | custom-call | tf_op jit(solution)/shard_map/pallas_call | solution.py:974

commit v4 on v3

--- a/solution.py
+++ b/solution.py
@@ -10,7 +10,7 @@
 norm_eps = 1e-06
 
 LANES = 128
-HALVES = 2
+HALVES = 4
 FEATURES = 48
 FOLDED = 16
 BLOCK = 1024
@@ -282,6 +282,139 @@
             passing(origin).wait_send()
 
     return start, receive, finish
+
+
+def flipped(chip, step, chips):
+    place, result = 1, 0
+    while place < chips:
+        bit = lax.rem(chip // place, 2)
+        result = result + place * ((1 - bit) if step // place % 2 else bit)
+        place *= 2
+    return result
+
+
+def weight_gather(source, weights, sent, far_sent, passed, far_passed, relayed, arrived, far_arrived):
+    group = lax.axis_index("grp")
+    shard = lax.axis_index("shard")
+    groups = lax.axis_size("grp")
+    chips = lax.axis_size("shard") // 2
+    chip = shard // 2
+    core = lax.rem(shard, 2)
+    partner = chip * 2 + 1 - core
+    rows, model = source.shape
+    quarter = model // groups
+    powers = [1 << b for b in range(chips.bit_length() - 1)]
+    near = [flipped(chip, step, chips) * 2 + core for step in powers]
+    far = [flipped(chip, s, chips) * 2 + core for s in range(1, chips) if s not in powers]
+    steps = [lax.rem(group + step, groups) for step in range(1, groups)]
+
+    def across(origin):
+        return origin + 1 - 2 * core
+
+    def whole(origin):
+        return weights.at[pl.ds(pl.multiple_of(origin * rows, rows), rows)]
+
+    def piece(origin, g):
+        return weights.at[
+            pl.ds(pl.multiple_of(origin * rows, rows), rows),
+            pl.ds(pl.multiple_of(g * quarter, quarter), quarter),
+        ]
+
+    def remote(src, dst, send_sem, recv_sem, to_group, to):
+        return pltpu.make_async_remote_copy(
+            src_ref=src,
+            dst_ref=dst,
+            send_sem=send_sem,
+            recv_sem=recv_sem,
+            device_id=(to_group, to),
+            device_id_type=MESH,
+        )
+
+    def near_to(other):
+        return remote(source, whole(shard), sent.at[other], arrived.at[shard], group, other)
+
+    def far_to(other):
+        mine = source.at[:, pl.ds(pl.multiple_of(group * quarter, quarter), quarter)]
+        return remote(
+            mine, piece(shard, group), far_sent.at[other], far_arrived.at[shard, group], group, other
+        )
+
+    def near_pass(origin):
+        return remote(
+            whole(origin), whole(origin), passed.at[origin], arrived.at[origin], group, partner
+        )
+
+    def far_pass(origin, g):
+        return remote(
+            piece(origin, g),
+            piece(origin, g),
+            far_passed.at[origin, g],
+            far_arrived.at[origin, g],
+            group,
+            partner,
+        )
+
+    def relay(origin, other):
+        return remote(
+            piece(origin, group),
+            piece(origin, group),
+            relayed.at[origin, other],
+            far_arrived.at[origin, group],
+            other,
+            shard,
+        )
+
+    def start_far():
+        for other in far:
+            far_to(other).start()
+
+    def start_near():
+        for other in near:
+            near_to(other).start()
+        near_to(partner).start()
+
+    def relay_far():
+        for origin in far:
+            far_pass(origin, group).wait_recv()
+            for other in steps:
+                relay(origin, other).start()
+            far_pass(origin, group).start()
+
+    def receive(use):
+        near_pass(partner).wait_recv()
+        use(partner)
+        for origin in near:
+            near_pass(origin).wait_recv()
+            near_pass(origin).start()
+            use(origin)
+        for origin in far:
+            for g in steps:
+                far_pass(origin, g).wait_recv()
+                far_pass(origin, g).start()
+            use(origin)
+        for origin in near:
+            near_pass(across(origin)).wait_recv()
+            use(across(origin))
+        for origin in far:
+            for g in range(groups):
+                far_pass(across(origin), g).wait_recv()
+            use(across(origin))
+
+    def finish():
+        for other in near:
+            near_to(other).wait_send()
+        near_to(partner).wait_send()
+        for other in far:
+            far_to(other).wait_send()
+        for origin in near:
+            near_pass(origin).wait_send()
+        for origin in far:
+            for g in range(groups):
+                far_pass(origin, g).wait_send()
+            for other in steps:
+                relay(origin, other).wait_send()
+
+    return start_far, start_near, relay_far, receive, finish
 
 
 def whole_kernel(
@@ -360,6 +493,10 @@
     weight_sent,
     weight_passed,
     weight_arrived,
+    far_sent,
+    far_passed,
+    far_relayed,
+    far_arrived,
     field_sent,
     field_passed,
     field_arrived,
@@ -432,9 +569,6 @@
             device_id_type=MESH,
         )
 
-    def weight_place(origin):
-        return weights.at[pl.ds(pl.multiple_of(origin * rows, rows), rows)]
-
     def weight_of(origin):
         return weights[pl.ds(pl.multiple_of(origin * rows, rows), rows), :]
 
@@ -442,8 +576,16 @@
     start_counts, receive_counts, finish_counts = messages(
         groups, shards, lambda other: count_row, landed_counts, count_sent, count_arrived
     )
-    start_weights, receive_weights, finish_weights = plane_gather(
-        weight_ref, weight_place, weight_sent, weight_passed, weight_arrived
+    start_far, start_near, relay_far, receive_weights, finish_weights = weight_gather(
+        weight_ref,
+        weights,
+        weight_sent,
+        far_sent,
+        weight_passed,
+        far_passed,
+        far_relayed,
+        weight_arrived,
+        far_arrived,
     )
     start_messages, receive_messages, finish_messages = messages(
         groups, shards, lambda other: message.at[other], landed, message_sent, message_arrived
@@ -452,13 +594,15 @@
         lead_own, lambda origin: leads.at[origin], lead_sent, lead_passed, lead_arrived
     )
     start_counts()
+    start_far()
     for other in others:
         turned_copy(other, shard).start()
-    start_weights()
+    start_near()
     landed_counts[me] = count_row[...]
     turned[shard] = turned_own[shard]
     weights[pl.ds(pl.multiple_of(shard * rows, rows), rows), :] = weight_ref[...]
 
+    relay_far()
     receive_counts()
     counts = landed_counts[:, 0, :]
     hot_lanes = jnp.min(jnp.where(counts == slots, 1, 0), axis=0, keepdims=True)
@@ -771,10 +915,11 @@
     start_gain, receive_gain, finish_gain = messages(
         groups, shards, lambda other: gain_row, landed_gain, gain_sent, gain_arrived
     )
-    gather_half(0)
-    gather_half(1)
-    sum_half(0)
-    sum_half(1)
+    for half in range(HALVES):
+        gather_half(half)
+        if half > 0:
+            sum_half(half - 1)
+    sum_half(HALVES - 1)
     landed_gain[me] = gain_row[...]
 
     token = iota((tokens, sent_rows), 0)
@@ -930,6 +1075,10 @@
             dma((shards,)),
             dma((shards,)),
             dma((shards,)),
+            dma((shards,)),
+            dma((shards, groups)),
+            dma((shards, groups)),
+            dma((shards, groups)),
             dma((HALVES, shards)),
             dma((HALVES, shards)),
             dma((HALVES, shards)),
@@ -955,36 +1104,53 @@
     return (colors, loss[0, 0], head_grad, gain.reshape(model), latent_grad)
 
 
-def hand_out_kernel(color_in, loss_in, head_in, gain_in, latent_in, color, loss, head, gain, latent):
-    color[...] = color_in[...]
-    loss[...] = loss_in[...]
-    gain[...] = gain_in[...]
-    head[...] = head_in[0].astype(jnp.float32)
-    latent[...] = latent_in[...]
+def hand_out_kernel(count, *refs):
+    sources, targets = refs[:count], refs[count : 2 * count]
+    buffers = refs[2 * count : 3 * count]
+    wide, arrived, left = refs[3 * count :]
+    inward = [
+        pltpu.make_async_copy(sources[i], buffers[i], arrived.at[i]) for i in range(count)
+    ]
+    for copy in inward:
+        copy.start()
+    outward = [
+        pltpu.make_async_copy(buffers[i], targets[i], left.at[i]) for i in range(1, count)
+    ]
+    groups, slice_rows, model = buffers[0].shape
+    inward[0].wait()
+    for g in range(groups):
+        rows = pl.ds(g * slice_rows, slice_rows)
+        wide[rows, :] = buffers[0][g].astype(jnp.float32)
+        outward.append(
+            pltpu.make_async_copy(wide.at[rows], targets[0].at[rows], left.at[count + g])
+        )
+        outward[-1].start()
+    for i in range(1, count):
+        inward[i].wait()
+        outward[i - 1].start()
+    for copy in outward:
+        copy.wait()
 
 
 def hand_out(colors, loss, head, gain, latent_grad):
     groups, slice_rows, model = head.shape
-    tokens = latent_grad.shape[0]
-    fixed = lambda i: (0, 0)
-    by_row = lambda i: (i, 0)
-    small = [pl.BlockSpec(colors.shape, fixed), pl.BlockSpec(loss.shape, fixed)]
-    gain_spec = pl.BlockSpec(gain.shape, fixed)
-    latent_spec = pl.BlockSpec((tokens // groups, model), by_row)
-    return pl.pallas_call(
-        hand_out_kernel,
-        grid=(groups,),
-        in_specs=small
-        + [pl.BlockSpec((1, slice_rows, model), lambda i: (i, 0, 0)), gain_spec, latent_spec],
-        out_specs=small + [pl.BlockSpec((slice_rows, model), by_row), gain_spec, latent_spec],
-        out_shape=[
-            jax.ShapeDtypeStruct(colors.shape, colors.dtype),
-            jax.ShapeDtypeStruct(loss.shape, loss.dtype),
-            jax.ShapeDtypeStruct((groups * slice_rows, model), jnp.float32),
-            jax.ShapeDtypeStruct(gain.shape, gain.dtype),
-            jax.ShapeDtypeStruct(latent_grad.shape, latent_grad.dtype),
+    values = [head, latent_grad, colors, loss, gain]
+    count = len(values)
+    full = jax.ShapeDtypeStruct((groups * slice_rows, model), jnp.float32)
+    anywhere = pl.BlockSpec(memory_space=pl.ANY)
+    head, latent_grad, colors, loss, gain = pl.pallas_call(
+        functools.partial(hand_out_kernel, count),
+        in_specs=[anywhere] * count,
+        out_specs=[anywhere] * count,
+        out_shape=[full] + [jax.ShapeDtypeStruct(v.shape, v.dtype) for v in values[1:]],
+        scratch_shapes=[pltpu.VMEM(v.shape, v.dtype) for v in values]
+        + [
+            pltpu.VMEM(full.shape, full.dtype),
+            pltpu.SemaphoreType.DMA((count,)),
+            pltpu.SemaphoreType.DMA((count + groups,)),
         ],
-    )(colors, loss, head, gain, latent_grad)
+    )(*values)
+    return colors, loss, head, gain, latent_grad
 
 
 def solution(mesh):

time: 71.5 us -> 69.7 us (0.975)
  Pallas kernels: 70.5 us -> 68.9 us
    pallas_call x1, Pallas kernels: 3.71 us -> 2.52 us  [hand_out(): pl.pallas_call(functools.partial(hand_out_kernel, count), in_specs=[anywh...]
where the time goes in v4:
time: 69.7 us; the launch traced here: 69.6 us
  Pallas kernels  68.9 us (99%)
    pallas_call x1, Pallas kernels, body(): pl.pallas_call(functools.partial(whole_kernel, groups, shards), in_specs=...  66.4 us
    pallas_call x1, Pallas kernels, hand_out(): pl.pallas_call(functools.partial(hand_out_kernel, count), in_specs=[anywh...  2.52 us

profile of v4, /device:TPU:0, one launch (start us, length us, event | category | flops | bytes accessed | tf_op | source)
XLA Modules:
  0.0 69.6 jit_solution(4158358988338842127)
XLA Ops:
  0.6 66.4 %shard_map.119 = (f32[3,64]{1,0:T(4,128)}, f32[1,1]{1,0:T(1,128)}, bf16[4,32,1024]{2,1,0:T(8,128)(2,1)}, f32[8,128]{1,0:T(8,128)}, bf16[128,1024]{1,0:T(8,128)(2,1)}) custom-call(bf16[128,1024]{1,0:T(8,128)(2,1)} %latent_ref.1, bf16[128,1024]{1,0:T(8,128)(2,1)} %weight_ref.1, bf16[4,32,1024]{2,1,0:T(8,128)(2,1)} %bitcast.6, f32[1,1024]{1,0:T(1,128)} %bitcast.7, ...), custom_call_target="tpu_custom_call" | custom-call | tf_op jit(solution)/shard_map/pallas_call | solution.py:1008
  67.1 2.5 %shard_map.120 = (f32[128,1024]{1,0:T(8,128)}, bf16[128,1024]{1,0:T(8,128)(2,1)}, f32[3,64]{1,0:T(4,128)}, f32[1,1]{1,0:T(1,128)}, f32[8,128]{1,0:T(8,128)}) custom-call(bf16[4,32,1024]{2,1,0:T(8,128)(2,1)} %get-tuple-element.15.refs_0_, bf16[128,1024]{1,0:T(8,128)(2,1)} %get-tuple-element.16.refs_1_, f32[3,64]{1,0:T(4,128)} %get-tuple-element.17.refs_2_, ...), custom_call_target="tpu_custom_call" | custom-call | tf_op jit(solution)/shard_map/pallas_call | solution.py:1141

commit v5 on v4

--- a/solution.py
+++ b/solution.py
@@ -13,6 +13,7 @@
 HALVES = 4
 FEATURES = 48
 FOLDED = 16
+LAG = 3
 BLOCK = 1024
 SINE = (3.14159265358979, -5.16771278004997, 2.55016403987735, -0.599264529320792, 0.0821458866111282, -0.00737043094571435, 0.000466302805767613, -0.0000219153534478303)
 MESH = pl.DeviceIdType.MESH
@@ -743,35 +744,6 @@
     set_weights(1, lead_field[0])
     lax.fori_loop(own_blocks, blocks, forward(1), 0)
     colors, losses = render_middle(ray_depth, raw, spacing, targets, factor, draw)
-    shade = jnp.where(
-        lane == 4 * slots + 4,
-        jnp.sum(losses, axis=(0, 1), keepdims=True) * (1.0 / ray_depth),
-        0.0,
-    )
-
-    def color_rows(start, stop):
-        columns = []
-        for side in (0, ray_depth):
-            values = jnp.zeros((stop - start, LANES), f32)
-            for c in range(3):
-                values = jnp.where(lane == c, colors[c][start:stop, side : side + 1], values)
-            columns.append(values)
-        return jnp.concatenate(columns, axis=0)
-
-    own_colors = color_rows(0, own_pairs)
-    hot_colors = color_rows(own_pairs, all_pairs)
-    back = select(keep, own_colors, (0, 0))
-    for j in range(slots):
-        part_back = back[j * total : (j + 1) * total]
-        shade = shade + (part_back if j == 0 else pltpu.roll(part_back, 4 * j, 1))
-    shade = shade + pltpu.roll(select(hot_keep, hot_colors, (0, 0)), 4 * slots, 1)
-    shades[:, 0, :] = shade
-    start_shades, receive_shades, finish_shades = messages(
-        groups, shards, lambda other: shades.at[other], landed_shades, shade_sent, shade_arrived
-    )
-    start_shades()
-    landed_shades[me] = shades[me]
-
     def backward(which):
         def step(i, carry):
             backward_block(
@@ -832,6 +804,36 @@
         for half in range(HALVES)
     ]
     gathers[0][0]()
+
+    shade = jnp.where(
+        lane == 4 * slots + 4,
+        jnp.sum(losses, axis=(0, 1), keepdims=True) * (1.0 / ray_depth),
+        0.0,
+    )
+
+    def color_rows(start, stop):
+        columns = []
+        for side in (0, ray_depth):
+            values = jnp.zeros((stop - start, LANES), f32)
+            for c in range(3):
+                values = jnp.where(lane == c, colors[c][start:stop, side : side + 1], values)
+            columns.append(values)
+        return jnp.concatenate(columns, axis=0)
+
+    own_colors = color_rows(0, own_pairs)
+    hot_colors = color_rows(own_pairs, all_pairs)
+    back = select(keep, own_colors, (0, 0))
+    for j in range(slots):
+        part_back = back[j * total : (j + 1) * total]
+        shade = shade + (part_back if j == 0 else pltpu.roll(part_back, 4 * j, 1))
+    shade = shade + pltpu.roll(select(hot_keep, hot_colors, (0, 0)), 4 * slots, 1)
+    shades[:, 0, :] = shade
+    start_shades, receive_shades, finish_shades = messages(
+        groups, shards, lambda other: shades.at[other], landed_shades, shade_sent, shade_arrived
+    )
+    start_shades()
+    landed_shades[me] = shades[me]
+
     piece_sum = hot_part[shard].astype(f32)
     for other in others:
         hot_copy(other, other).wait_recv()
@@ -917,9 +919,10 @@
     )
     for half in range(HALVES):
         gather_half(half)
-        if half > 0:
-            sum_half(half - 1)
-    sum_half(HALVES - 1)
+        if half >= LAG:
+            sum_half(half - LAG)
+    for half in range(HALVES - LAG, HALVES):
+        sum_half(half)
     landed_gain[me] = gain_row[...]
 
     token = iota((tokens, sent_rows), 0)

time: 69.7 us -> 67.7 us (0.971)
  Pallas kernels: 68.9 us -> 66.9 us
    pallas_call x1, Pallas kernels: 66.4 us -> 64.4 us  [body(): pl.pallas_call(functools.partial(whole_kernel, groups, shards), in_specs=...]
where the time goes in v5:
time: 67.7 us; the launch traced here: 67.6 us
  Pallas kernels  66.9 us (99%)
    pallas_call x1, Pallas kernels, body(): pl.pallas_call(functools.partial(whole_kernel, groups, shards), in_specs=...  64.4 us
    pallas_call x1, Pallas kernels, hand_out(): pl.pallas_call(functools.partial(hand_out_kernel, count), in_specs=[anywh...  2.52 us

profile of v5, /device:TPU:0, one launch (start us, length us, event | category | flops | bytes accessed | tf_op | source)
XLA Modules:
  0.0 67.6 jit_solution(1279467931291658239)
XLA Ops:
  0.6 64.4 %shard_map.119 = (f32[3,64]{1,0:T(4,128)}, f32[1,1]{1,0:T(1,128)}, bf16[4,32,1024]{2,1,0:T(8,128)(2,1)}, f32[8,128]{1,0:T(8,128)}, bf16[128,1024]{1,0:T(8,128)(2,1)}) custom-call(bf16[128,1024]{1,0:T(8,128)(2,1)} %latent_ref.1, bf16[128,1024]{1,0:T(8,128)(2,1)} %weight_ref.1, bf16[4,32,1024]{2,1,0:T(8,128)(2,1)} %bitcast.6, f32[1,1024]{1,0:T(1,128)} %bitcast.7, ...), custom_call_target="tpu_custom_call" | custom-call | tf_op jit(solution)/shard_map/pallas_call | solution.py:1011
  65.0 2.5 %shard_map.120 = (f32[128,1024]{1,0:T(8,128)}, bf16[128,1024]{1,0:T(8,128)(2,1)}, f32[3,64]{1,0:T(4,128)}, f32[1,1]{1,0:T(1,128)}, f32[8,128]{1,0:T(8,128)}) custom-call(bf16[4,32,1024]{2,1,0:T(8,128)(2,1)} %get-tuple-element.15.refs_0_, bf16[128,1024]{1,0:T(8,128)(2,1)} %get-tuple-element.16.refs_1_, f32[3,64]{1,0:T(4,128)} %get-tuple-element.17.refs_2_, ...), custom_call_target="tpu_custom_call" | custom-call | tf_op jit(solution)/shard_map/pallas_call | solution.py:1144

commit v6 on v5

--- a/solution.py
+++ b/solution.py
@@ -418,9 +418,51 @@
     return start_far, start_near, relay_far, receive, finish
 
 
+INPUTS = 10
+
+
+def staged_kernel(groups, shards, *refs):
+    wait_all = greet_all(groups, shards)
+    sources, color, loss, grad, gain, latent = refs[:INPUTS], *refs[INPUTS : INPUTS + 5]
+    rest = refs[INPUTS + 5 :]
+    latent_buffer, buffers, arrived, left = rest[0], rest[1 : INPUTS + 1], *rest[-2:]
+    inward = [
+        pltpu.make_async_copy(sources[i], buffers[i], arrived.at[i]) for i in range(INPUTS)
+    ]
+    for copy in inward:
+        copy.start()
+
+    def latent_out():
+        return pltpu.make_async_copy(latent_buffer, latent, left.at[HALVES])
+
+    def grad_out(half, values):
+        columns = values.shape[-1]
+        strip = grad.at[:, :, half * columns : (half + 1) * columns]
+        return pltpu.make_async_copy(values, strip, left.at[half])
+
+    for copy in inward:
+        copy.wait()
+    whole_kernel(
+        groups,
+        shards,
+        wait_all,
+        latent_out,
+        grad_out,
+        *buffers,
+        color,
+        loss,
+        gain,
+        latent_buffer,
+        *rest[INPUTS + 1 : -2],
+    )
+
+
 def whole_kernel(
     groups,
     shards,
+    wait_all,
+    latent_out,
+    grad_out,
     latent_ref,
     weight_ref,
     weight_part_ref,
@@ -433,7 +475,6 @@
     scene_ref,
     color_ref,
     loss_ref,
-    grad_ref,
     gain_grad_ref,
     latent_grad_ref,
     count_row,
@@ -525,8 +566,6 @@
     f32 = jnp.float32
     bf16 = jnp.bfloat16
 
-    wait_all = greet_all(groups, shards)
-
     latent = latent_ref[...].astype(f32)
     inv_rms = lax.rsqrt(jnp.mean(latent * latent, axis=1, keepdims=True) + norm_eps)
     x_norm = (latent * inv_rms * gain_ref[...]).astype(bf16)
@@ -940,6 +979,7 @@
         inv_rms * (d_scaled - x_hat * jnp.mean(d_scaled * x_hat, axis=1, keepdims=True))
     ).astype(bf16)
 
+    latent_out().start()
     receive_shades()
     returned = landed_shades[:, 0, :]
     loss_ref[...] = jnp.sum(
@@ -954,15 +994,17 @@
         )
 
     for half in range(HALVES):
-        grad_ref[group, :, half * columns : (half + 1) * columns] = done[half, group]
         for other in group_steps:
             done_copy(half, other, other).wait_recv()
-            grad_ref[other, :, half * columns : (half + 1) * columns] = done[half, other]
+        grad_out(half, done.at[half]).start()
     receive_gain()
     gains = landed_gain[:, 0, :slice_rows]
     gains = jnp.concatenate([gains[g * shards : (g + 1) * shards] for g in range(groups)], axis=1)
     gain_grad_ref[...] = gains / gain_rows_ref[...]
 
+    latent_out().wait()
+    for half in range(HALVES):
+        grad_out(half, done.at[half]).wait()
     finish_counts()
     finish_weights()
     finish_messages()
@@ -1008,10 +1050,23 @@
     dma = pltpu.SemaphoreType.DMA
     f32, bf16 = jnp.float32, jnp.bfloat16
     vmem = pltpu.VMEM
+    anywhere = pl.BlockSpec(memory_space=pl.ANY)
+    inputs = (
+        latents,
+        head_weight,
+        head_weight.reshape(groups, slice_rows, model),
+        norm_gain.reshape(1, model),
+        norm_gain.reshape(shards, rows),
+        color_head,
+        sample_points,
+        sample_spacing,
+        ray_targets,
+        ray_scene.reshape(1, ray_count),
+    )
     colors, loss, head, gain, latent_grad = pl.pallas_call(
-        functools.partial(whole_kernel, groups, shards),
-        in_specs=[in_vmem] * 10,
-        out_specs=[in_vmem] * 5,
+        functools.partial(staged_kernel, groups, shards),
+        in_specs=[anywhere] * INPUTS,
+        out_specs=[in_vmem, in_vmem, anywhere, in_vmem, anywhere],
         out_shape=[
             jax.ShapeDtypeStruct((3, ray_count), f32),
             jax.ShapeDtypeStruct((1, 1), f32),
@@ -1019,7 +1074,9 @@
             jax.ShapeDtypeStruct((shards, rows), f32),
             jax.ShapeDtypeStruct((tokens, model), bf16),
         ],
-        scratch_shapes=[
+        scratch_shapes=[vmem((tokens, model), bf16)]
+        + [vmem(value.shape, value.dtype) for value in inputs]
+        + [
             vmem((1, LANES), f32),
             vmem((devices, 1, LANES), f32),
             vmem((rows, fold_rows), bf16),
@@ -1089,20 +1146,11 @@
             dma((HALVES, groups)),
             dma((HALVES, groups)),
             dma((HALVES, groups)),
+            dma((INPUTS,)),
+            dma((HALVES + 1,)),
         ],
         compiler_params=pltpu.CompilerParams(collective_id=1, has_side_effects=True),
-    )(
-        latents,
-        head_weight,
-        head_weight.reshape(groups, slice_rows, model),
-        norm_gain.reshape(1, model),
-        norm_gain.reshape(shards, rows),
-        color_head,
-        sample_points,
-        sample_spacing,
-        ray_targets,
-        ray_scene.reshape(1, ray_count),
-    )
+    )(*inputs)
     colors, loss, head_grad, gain, latent_grad = hand_out(colors, loss, head, gain, latent_grad)
     return (colors, loss[0, 0], head_grad, gain.reshape(model), latent_grad)
 

time: 67.7 us -> 66.7 us (0.985)
  Pallas kernels: 66.9 us -> 65.9 us
    pallas_call x1, Pallas kernels: 64.4 us -> 63.4 us  [body(): pl.pallas_call(functools.partial(staged_kernel, groups, shards), in_specs...]
where the time goes in v6:
time: 66.7 us; the launch traced here: 66.6 us
  Pallas kernels  65.9 us (99%)
    pallas_call x1, Pallas kernels, body(): pl.pallas_call(functools.partial(staged_kernel, groups, shards), in_specs...  63.4 us
    pallas_call x1, Pallas kernels, hand_out(): pl.pallas_call(functools.partial(hand_out_kernel, count), in_specs=[anywh...  2.52 us

profile of v6, /device:TPU:0, one launch (start us, length us, event | category | flops | bytes accessed | tf_op | source)
XLA Modules:
  0.0 66.6 jit_solution(5180286867875933350)
XLA Ops:
  0.6 63.4 %shard_map.119 = (f32[3,64]{1,0:T(4,128)}, f32[1,1]{1,0:T(1,128)}, bf16[4,32,1024]{2,1,0:T(8,128)(2,1)}, f32[8,128]{1,0:T(8,128)}, bf16[128,1024]{1,0:T(8,128)(2,1)}) custom-call(bf16[128,1024]{1,0:T(8,128)(2,1)} %refs_0_.1, bf16[128,1024]{1,0:T(8,128)(2,1)} %refs_1_.1, bf16[4,32,1024]{2,1,0:T(8,128)(2,1)} %bitcast.6, f32[1,1024]{1,0:T(1,128)} %bitcast.7, ...), custom_call_target="tpu_custom_call" | custom-call | tf_op jit(solution)/shard_map/pallas_call | solution.py:1066
  64.0 2.5 %shard_map.120 = (f32[128,1024]{1,0:T(8,128)}, bf16[128,1024]{1,0:T(8,128)(2,1)}, f32[3,64]{1,0:T(4,128)}, f32[1,1]{1,0:T(1,128)}, f32[8,128]{1,0:T(8,128)}) custom-call(bf16[4,32,1024]{2,1,0:T(8,128)(2,1)} %get-tuple-element.15.refs_0_, bf16[128,1024]{1,0:T(8,128)(2,1)} %get-tuple-element.16.refs_1_, f32[3,64]{1,0:T(4,128)} %get-tuple-element.17.refs_2_, ...), custom_call_target="tpu_custom_call" | custom-call | tf_op jit(solution)/shard_map/pallas_call | solution.py:1192

commit v7 on v6

--- a/solution.py
+++ b/solution.py
@@ -13,7 +13,7 @@
 HALVES = 4
 FEATURES = 48
 FOLDED = 16
-LAG = 3
+LAG = 4
 BLOCK = 1024
 SINE = (3.14159265358979, -5.16771278004997, 2.55016403987735, -0.599264529320792, 0.0821458866111282, -0.00737043094571435, 0.000466302805767613, -0.0000219153534478303)
 MESH = pl.DeviceIdType.MESH

time: 66.7 us -> 66.7 us (level)
  no operation moved by 1% of the time
where the time goes in v7:
time: 66.7 us; the launch traced here: 66.6 us
  Pallas kernels  65.9 us (99%)
    pallas_call x1, Pallas kernels, body(): pl.pallas_call(functools.partial(staged_kernel, groups, shards), in_specs...  63.4 us
    pallas_call x1, Pallas kernels, hand_out(): pl.pallas_call(functools.partial(hand_out_kernel, count), in_specs=[anywh...  2.52 us

profile of v7, /device:TPU:0, one launch (start us, length us, event | category | flops | bytes accessed | tf_op | source)
XLA Modules:
  0.0 66.6 jit_solution(5180286867875933350)
XLA Ops:
  0.6 63.4 %shard_map.119 = (f32[3,64]{1,0:T(4,128)}, f32[1,1]{1,0:T(1,128)}, bf16[4,32,1024]{2,1,0:T(8,128)(2,1)}, f32[8,128]{1,0:T(8,128)}, bf16[128,1024]{1,0:T(8,128)(2,1)}) custom-call(bf16[128,1024]{1,0:T(8,128)(2,1)} %refs_0_.1, bf16[128,1024]{1,0:T(8,128)(2,1)} %refs_1_.1, bf16[4,32,1024]{2,1,0:T(8,128)(2,1)} %bitcast.6, f32[1,1024]{1,0:T(1,128)} %bitcast.7, ...), custom_call_target="tpu_custom_call" | custom-call | tf_op jit(solution)/shard_map/pallas_call | solution.py:1066
  64.0 2.5 %shard_map.120 = (f32[128,1024]{1,0:T(8,128)}, bf16[128,1024]{1,0:T(8,128)(2,1)}, f32[3,64]{1,0:T(4,128)}, f32[1,1]{1,0:T(1,128)}, f32[8,128]{1,0:T(8,128)}) custom-call(bf16[4,32,1024]{2,1,0:T(8,128)(2,1)} %get-tuple-element.15.refs_0_, bf16[128,1024]{1,0:T(8,128)(2,1)} %get-tuple-element.16.refs_1_, f32[3,64]{1,0:T(4,128)} %get-tuple-element.17.refs_2_, ...), custom_call_target="tpu_custom_call" | custom-call | tf_op jit(solution)/shard_map/pallas_call | solution.py:1192
